TPU v7x, 256 devices: a whole 4x4x8 slice. The times are simulated.
256 devices in a mesh: grp: 16 (over y_hi, x, core), pose: 16 (over y_lo, z).
Axes of the slice: x: 4, y: 4 (y_hi: 2, y_lo: 2; y = y_hi * 2 + y_lo), z: 8, core: 2. Of those that a mesh axis runs over, the one named last changes fastest.
Arguments:
- particles: bfloat16 [81920, 16384], P(('grp', 'pose')), may hold values from -64 to 64
- projections: bfloat16 [128, 16384], P('pose'), may hold values from -1.5 to 1.5
- ctf_table: bfloat16 [32, 16384], replicated, may hold values from 0.099609375 to 1
- group_ids: int32 [81920], P(('grp', 'pose')), may hold values from 0 to 31
Outputs:
- gradient: float32 [128, 16384], P('pose', 'grp')
- log_norm: float32 [81920], P(('grp', 'pose'))
All inputs are finite; a program needn't handle non-finite values.
Results may differ from a plain program's by a relative error of at most 0.0065.
Values may be sent and summed in bfloat16 or wider, within the bound.
No kernel may reach another device: no remote copies, remote signals or barrier semaphores. Data moves between devices by JAX's collectives and lax.ppermute only.
A program may use at most 128 MiB of HBM per device.

v0:
```python
import math

import jax
import jax.numpy as jnp
from jax import lax
from jax.sharding import PartitionSpec as P


def shards(particles, projections, ctf_table, group_ids):
    high = lax.Precision.HIGHEST
    part_count = particles.shape[0]
    feature_count = particles.shape[1]
    group_count = ctf_table.shape[0]
    pose_local = projections.shape[0]
    pose_total = pose_local * lax.axis_size("pose")
    particle_total = part_count * lax.axis_size("grp") * lax.axis_size("pose")
    inverse = 4.0 / math.sqrt(feature_count)
    factor = pose_total / particle_total
    one_hot = (group_ids[:, None] == jnp.arange(group_count, dtype=jnp.int32)[None, :]).astype(
        jnp.bfloat16
    )
    one_hot_f32 = one_hot.astype(jnp.float32)
    ctf_rows = jnp.dot(one_hot, ctf_table, preferred_element_type=jnp.bfloat16)
    weighted = ctf_rows * particles
    ctf_square = jnp.square(ctf_table.astype(jnp.float32))
    gathered = lax.all_gather(projections, "pose", axis=0, tiled=True)
    raw_dots = lax.dot_general(
        weighted, gathered, (((1,), (1,)), ((), ())), preferred_element_type=jnp.float32
    )
    model_f32 = gathered.astype(jnp.float32)
    norms = lax.dot_general(
        ctf_square,
        model_f32 * model_f32,
        (((1,), (1,)), ((), ())),
        precision=high,
        preferred_element_type=jnp.float32,
    )
    picked = jnp.dot(one_hot_f32, norms, precision=high)
    scores = inverse * (raw_dots - 0.5 * picked)
    row_peak = jnp.max(scores, axis=1, keepdims=True)
    log_norm = row_peak[:, 0] + jnp.log(jnp.sum(jnp.exp(scores - row_peak), axis=1))
    weights = jnp.exp(scores - log_norm[:, None]).astype(jnp.bfloat16)
    pose_mass = lax.dot_general(
        weights, one_hot, (((0,), (0,)), ((), ())), preferred_element_type=jnp.float32
    )
    numerator = lax.dot_general(
        weights, weighted, (((0,), (0,)), ((), ())), preferred_element_type=jnp.float32
    )
    model_rows = gathered.astype(jnp.float32)
    numerator = numerator - model_rows * jnp.dot(pose_mass, ctf_square, precision=high)
    pose_share = lax.psum_scatter(factor * numerator, "pose", scatter_dimension=0, tiled=True)
    out_block = lax.psum_scatter(pose_share, "grp", scatter_dimension=1, tiled=True)
    return (out_block, log_norm)


def solution(mesh):
    return jax.shard_map(
        shards,
        mesh=mesh,
        in_specs=(P(("grp", "pose"), None), P("pose", None), P(), P(("grp", "pose"))),
        out_specs=(P("pose", "grp"), P(("grp", "pose"))),
        check_vma=False,
    )
```

profile of v0, /device:TPU:2, one launch (start us, length us, event | category | flops | bytes accessed | tf_op | source)
XLA Modules:
  0.0 300.7 jit_solution(8398676469700784404)
XLA Ops:
  7.2 0.0 all-gather.2.cloned.1.call-start
  7.2 0.7 all-gather.2.cloned.1.call-update
  7.9 0.0 copy-start.1
  7.9 0.0 reduce-scatter.3.cloned.1.call-start
  8.0 9.7 %convolution_multiply_fusion.1 = bf16[320,16384]{1,0:T(8,128)(2,1)} fusion(bf16[320,16384]{1,0:T(8,128)(2,1)} %param.4, bf16[32,16384]{1,0:T(8,128)(2,1)} %param.6, s32[320]{0:T(512)} %param.7), kind=kOutput, calls=%fused_computation.3 | convolution fusion | flops 340797440 | bytes 22021376 | tf_op jit(solution)/shard_map/dot_general | solution.py:23
  17.7 72.0 %all-gather.2.cloned.1.call-done = bf16[128,16384]{1,0:T(8,128)(2,1)} async-done(((bf16[8,16384]{1,0:T(8,128)(2,1)}), bf16[128,16384]{1,0:T(8,128)(2,1)}) %all-gather.2.cloned.1.call-update) | async-done | bytes 4194320 | tf_op jit(solution)/shard_map/all_gather | solution.py:26
  89.6 0.0 copy-done.1
  89.6 0.0 slice-start
  89.6 10.0 %fusion.2 = f32[32,128]{1,0:T(8,128)S(1)} fusion(bf16[128,16384]{1,0:T(8,128)(2,1)} %all-gather.2.cloned.1.call-done, bf16[32,16384]{1,0:T(8,128)(2,1)S(1)} %copy-done.1), kind=kOutput, calls=%fused_computation.5 | convolution fusion | flops 810549248 | bytes 5259264 | tf_op jit(solution)/shard_map/dot_general | solution.py:31
  99.6 0.0 copy-start.2
  99.6 0.0 slice-start.1
  99.6 0.0 slice-start.2
  99.7 7.0 %fusion.11 = f32[320,128]{1,0:T(8,128)S(1)} fusion(bf16[320,16384]{1,0:T(8,128)(2,1)} %convolution_multiply_fusion.1, bf16[128,16384]{1,0:T(8,128)(2,1)} %all-gather.2.cloned.1.call-done), kind=kOutput, calls=%fused_computation.20 | convolution fusion | flops 1342177280 | bytes 14843904 | tf_op jit(solution)/shard_map/dot_general | solution.py:27
  106.6 0.0 copy-done.2
  106.6 0.4 fusion.10
  107.0 0.2 exponential_reduce_fusion
  107.3 0.0 slice-done
  107.3 0.0 slice-done.1
  107.3 0.0 slice-done.2
  107.3 0.0 copy-start.3
  107.3 0.0 copy-start
  107.3 2.5 fusion.9
  109.8 0.0 copy-done.3
  109.8 0.3 fusion.5
  110.1 0.0 copy-done
  110.1 10.2 %fusion.1 = f32[128,16384]{1,0:T(8,128)} fusion(f32[128,16384]{1,0:T(8,128)S(1)} %fusion.9, f32[128,32]{1,0:T(8,128)S(1)} %fusion.5, bf16[128,16384]{1,0:T(8,128)(2,1)S(1)} %copy-done, bf16[32,16384]{1,0:T(8,128)(2,1)S(1)} %copy-done.1), kind=kOutput, calls=%fused_computation.2 | convolution fusion | flops 814743552 | bytes 22036480 | tf_op jit(solution)/shard_map/dot_general | solution.py:50
  120.4 0.0 reduce-scatter.3.cloned.1.call-update
  120.4 0.0 reduce-scatter.5.cloned.1.call-start
  120.4 98.7 %reduce-scatter.3.cloned.1.call-done = f32[8,16384]{1,0:T(8,128)} async-done(((f32[128,16384]{1,0:T(8,128)}), f32[8,16384]{1,0:T(8,128)}) %reduce-scatter.3.cloned.1.call-update) | async-done | bytes 524304 | tf_op jit(solution)/shard_map/reduce_scatter | solution.py:51
  219.1 0.0 reduce-scatter.5.cloned.1.call-update
  219.1 75.0 %reduce-scatter.5.cloned.1.call-done = f32[8,1024]{1,0:T(8,128)} async-done(((f32[8,16384]{1,0:T(8,128)}), f32[8,1024]{1,0:T(8,128)}) %reduce-scatter.5.cloned.1.call-update) | async-done | bytes 32784 | tf_op jit(solution)/shard_map/reduce_scatter | solution.py:52
  (2 shorter events, 0.0 us)
Async XLA Ops:
  7.2 82.5 %all-gather.2.cloned.1.call-start = ((), (), s32[]{:S(2)}) async-start(), calls=%async_computation.2 | async-start | bytes 4456448 | tf_op jit(solution)/shard_map/all_gather | solution.py:26
  7.9 81.7 %copy-start.1 = (bf16[32,16384]{1,0:T(8,128)(2,1)S(1)}, bf16[32,16384]{1,0:T(8,128)(2,1)}, u32[]{:S(2)}) copy-start(bf16[32,16384]{1,0:T(8,128)(2,1)} %param.6) | copy-start | bytes 3145732
  7.9 211.2 %reduce-scatter.3.cloned.1.call-start = ((), (), s32[]{:S(2)}) async-start(), calls=%async_computation.3 | async-start | bytes 8912896 | tf_op jit(solution)/shard_map/reduce_scatter | solution.py:51
  89.6 17.6 %slice-start = ((s8[10485760]{0:T(1024)(128)(4,1)}), s8[4194304]{0:T(1024)(128)(4,1)S(1)}, s32[]{:S(2)}) async-start(s8[10485760]{0:T(1024)(128)(4,1)} %bitcast.6), calls=%async_computation.5 | async-start | bytes 8388608
  99.6 7.0 %copy-start.2 = (s32[320]{0:T(512)S(1)}, s32[320]{0:T(512)}, u32[]{:S(2)}) copy-start(s32[320]{0:T(512)} %param.7) | copy-start | bytes 3844
  99.6 7.6 %slice-start.1 = ((s8[10485760]{0:T(1024)(128)(4,1)}), s8[4194304]{0:T(1024)(128)(4,1)S(1)}, s32[]{:S(2)}) async-start(s8[10485760]{0:T(1024)(128)(4,1)} %bitcast.6), calls=%async_computation.6 | async-start | bytes 8388608
  99.6 7.6 %slice-start.2 = ((s8[10485760]{0:T(1024)(128)(4,1)}), s8[2097152]{0:T(1024)(128)(4,1)S(1)}, s32[]{:S(2)}) async-start(s8[10485760]{0:T(1024)(128)(4,1)} %bitcast.6), calls=%async_computation.7 | async-start | bytes 4194304
  107.3 2.5 copy-start.3
  107.3 2.8 copy-start
  120.4 173.8 %reduce-scatter.5.cloned.1.call-start = ((), (), s32[]{:S(2)}) async-start(), calls=%async_computation.4 | async-start | bytes 557056 | tf_op jit(solution)/shard_map/reduce_scatter | solution.py:52
Sparse Core Ops, SparseCore 0:
  9.8 79.7 all-gather.1
  120.5 98.5 reduce-scatter.2
  223.8 70.3 reduce-scatter.4
where the time goes:
time: 301 us
  waiting for transfers between devices  246 us (82%)
  matrix products  40 us (13%)
  between operations  13.9 us (5%)
    reduce_scatter x1, waiting for transfers between devices, shards(): lax.psum_scatter(factor * numerator, 'pose', scatter_dimension=0, tiled=T...  98.7 us
    reduce_scatter x1, waiting for transfers between devices, shards(): lax.psum_scatter(pose_share, 'grp', scatter_dimension=1, tiled=True)  75 us
    all_gather x1, waiting for transfers between devices, shards(): gathered = lax.all_gather(projections, 'pose', axis=0, tiled=True)  72 us
    dot_general x1, matrix products, shards(): jnp.dot(pose_mass, ctf_square, precision=high)  10.2 us
    dot_general x1, matrix products, shards(): lax.dot_general(ctf_square, model_f32 * model_f32, (((1,), (1,)), ((), ()...  9.99 us
    dot_general x1, matrix products, shards(): ctf_rows = jnp.dot(one_hot, ctf_table, preferred_element_type=jnp.bfloat16)  9.71 us
    dot_general x1, matrix products, shards(): lax.dot_general(weighted, gathered, (((1,), (1,)), ((), ())), preferred_e...  6.95 us
  transfers between devices with their start and end apart: 3, of which 3 were waited for; matrix products, arithmetic and copies ran while one was open for 3% of the time, Pallas kernels for 0%

commit v1 on v0

v1 whole, which is shorter than its diff:
```python
import functools
import math

import jax
import jax.numpy as jnp
from jax import lax
from jax.experimental import pallas as pl
from jax.experimental.pallas import tpu as pltpu
from jax.sharding import PartitionSpec as P

NAMES = ("yh", "x", "core", "yl", "z")
BLK = 1024
BF = jnp.bfloat16
F32 = jnp.float32


def dot_tn(a, b):
    return lax.dot_general(a, b, (((0,), (0,)), ((), ())), preferred_element_type=F32)


def dot_nt(a, b):
    return lax.dot_general(a, b, (((1,), (1,)), ((), ())), preferred_element_type=F32)


def one_hot_t(ids, groups):
    rows = lax.broadcasted_iota(jnp.int32, (groups, ids.shape[1]), 0)
    return jnp.where(rows == ids, 1.0, 0.0).astype(BF)


def split2(v):
    hi = v.astype(BF)
    return hi, (v - hi.astype(F32)).astype(BF)


def split3(v):
    hi = v.astype(BF)
    rest = v - hi.astype(F32)
    mid = rest.astype(BF)
    return hi, mid, (rest - mid.astype(F32)).astype(BF)


def weighted_kernel(par_ref, ids_ref, ctf_ref, part_ref, out_ref):
    hot = one_hot_t(ids_ref[...], ctf_ref.shape[0])
    rows = dot_tn(hot, ctf_ref[...])
    out_ref[...] = (rows * part_ref[...].astype(F32)).astype(BF)


def weighted_call(parity, ids, ctf, particles):
    n, f = particles.shape
    g = ctf.shape[0]
    nb = f // BLK // 2
    return pl.pallas_call(
        weighted_kernel,
        grid_spec=pltpu.PrefetchScalarGridSpec(
            num_scalar_prefetch=1,
            grid=(nb,),
            in_specs=[
                pl.BlockSpec((1, n), lambda j, p: (0, 0)),
                pl.BlockSpec((g, BLK), lambda j, p: (0, 2 * j + p[0])),
                pl.BlockSpec((n, BLK), lambda j, p: (0, 2 * j + p[0])),
            ],
            out_specs=pl.BlockSpec((n, BLK), lambda j, p: (0, j)),
        ),
        out_shape=jax.ShapeDtypeStruct((n, f // 2), BF),
    )(parity, ids, ctf, particles)


def score_kernel(par_ref, wa_ref, wb_ref, proj_ref, ctf_ref, s_ref, n_ref):
    j = pl.program_id(0)
    n = wa_ref.shape[0]
    g = ctf_ref.shape[0]
    proj = proj_ref[...]
    poses = proj.shape[0]
    da = dot_nt(wa_ref[...], proj)
    db = dot_nt(wb_ref[...], proj)
    c = ctf_ref[...].astype(F32)
    pf = proj.astype(F32)
    ch, cl = split2(c * c)
    ph, plo = split2(pf * pf)
    quad = dot_nt(jnp.concatenate([ch, cl], axis=0), jnp.concatenate([ph, plo], axis=0))
    dn = (quad[:g, :poses] + quad[g:, :poses]) + (quad[:g, poses:] + quad[g:, poses:])

    @pl.when(j == 0)
    def _():
        s_ref[:n, :] = da
        s_ref[n:, :] = db
        n_ref[...] = dn

    @pl.when(j > 0)
    def _():
        s_ref[:n, :] += da
        s_ref[n:, :] += db
        n_ref[...] += dn


def score_call(parity, wa, wb, proj, ctf):
    n, f = wa.shape
    g = ctf.shape[0]
    poses = proj.shape[0]
    return pl.pallas_call(
        score_kernel,
        grid_spec=pltpu.PrefetchScalarGridSpec(
            num_scalar_prefetch=1,
            grid=(f // BLK,),
            in_specs=[
                pl.BlockSpec((n, BLK), lambda j, p: (0, j)),
                pl.BlockSpec((n, BLK), lambda j, p: (0, j)),
                pl.BlockSpec((poses, BLK), lambda j, p: (0, j)),
                pl.BlockSpec((g, BLK), lambda j, p: (0, 2 * j + p[0])),
            ],
            out_specs=[
                pl.BlockSpec((2 * n, poses), lambda j, p: (0, 0)),
                pl.BlockSpec((g, poses), lambda j, p: (0, 0)),
            ],
        ),
        out_shape=[
            jax.ShapeDtypeStruct((2 * n, poses), F32),
            jax.ShapeDtypeStruct((g, poses), F32),
        ],
    )(parity, wa, wb, proj, ctf)


def softmax_kernel(inverse, ids_ref, *refs):
    s0, r0, s1, r1, n0, m0, n1, m1, log_ref, w_ref, mass_ref = refs
    g = n0.shape[0]
    raw = jnp.concatenate([s0[...] + r0[...], s1[...] + r1[...]], axis=1)
    norms = jnp.concatenate([n0[...] + m0[...], n1[...] + m1[...]], axis=1)
    hot = one_hot_t(ids_ref[...], g)
    picked = dot_tn(jnp.concatenate([hot, hot, hot], axis=0), jnp.concatenate(split3(norms), axis=0))
    scores = inverse * (raw - 0.5 * picked)
    peak = jnp.max(scores, axis=1, keepdims=True)
    log_norm = peak + jnp.log(jnp.sum(jnp.exp(scores - peak), axis=1, keepdims=True))
    weights = jnp.exp(scores - log_norm).astype(BF)
    log_ref[...] = log_norm[: log_ref.shape[0], :]
    w_ref[...] = weights
    mass_ref[...] = jnp.dot(hot, weights, preferred_element_type=F32)


def softmax_call(inverse, ids, parts):
    rows = ids.shape[1]
    poses = 2 * parts[0].shape[1]
    g = parts[4].shape[0]
    return pl.pallas_call(
        functools.partial(softmax_kernel, inverse),
        out_shape=[
            jax.ShapeDtypeStruct((rows // 2, 1), F32),
            jax.ShapeDtypeStruct((rows, poses), BF),
            jax.ShapeDtypeStruct((g, poses), F32),
        ],
    )(ids, *parts)


def gradient_kernel(by_y, jt_ref, w_ref, mass_ref, wa_ref, wb_ref, p0_ref, p1_ref, ctf_ref, *outs):
    s = pl.program_id(0)
    a, dx = s // 4, s % 4
    n = wa_ref.shape[0]
    acc = dot_tn(w_ref[:n, :], wa_ref[...]) + dot_tn(w_ref[n:, :], wb_ref[...])
    c = ctf_ref[...].astype(F32)
    ch, cl = split2(c * c)
    mh, mm, ml = split3(mass_ref[...])
    corr = dot_tn(
        jnp.concatenate([mh, mh, mm, mm, ml], axis=0), jnp.concatenate([ch, cl, ch, cl, ch], axis=0)
    )
    half = p0_ref.shape[0]
    top = acc[:half] - p0_ref[...].astype(F32) * corr[:half]
    low = acc[half:] - p1_ref[...].astype(F32) * corr[half:]
    if by_y:
        for at in range(2):

            @pl.when(a == at)
            def _(at=at):
                for b, v in ((0, top), (1, low)):
                    ref = outs[2 * at + b]
                    ref[dx] = v.astype(ref.dtype)
    else:
        for at in range(4):

            @pl.when(dx == at)
            def _(at=at):
                ref = outs[at]
                ref[a, 0] = top.astype(ref.dtype)
                ref[a, 1] = low.astype(ref.dtype)


def gradient_call(by_y, jt, weights, mass, wa, wb, p0, p1, ctf):
    n, f = wa.shape
    g = ctf.shape[0]
    half = p0.shape[0]
    col = BLK // 2
    h = 0 if by_y else 1
    lead = (4,) if by_y else (2, 2)
    outs = [jax.ShapeDtypeStruct(lead + (half, col), F32 if i == 0 else BF) for i in range(4)]
    full = pl.BlockSpec(lead + (half, col), lambda s, t: (0,) * (len(lead) + 2))
    return pl.pallas_call(
        functools.partial(gradient_kernel, by_y),
        grid_spec=pltpu.PrefetchScalarGridSpec(
            num_scalar_prefetch=1,
            grid=(8,),
            in_specs=[
                pl.BlockSpec((2 * n, 2 * half), lambda s, t: (0, 0)),
                pl.BlockSpec((g, 2 * half), lambda s, t: (0, 0)),
                pl.BlockSpec((n, col), lambda s, t: (0, 2 * t[s] + h)),
                pl.BlockSpec((n, col), lambda s, t: (0, 2 * t[s] + h)),
                pl.BlockSpec((half, col), lambda s, t: (0, 2 * t[s] + h)),
                pl.BlockSpec((half, col), lambda s, t: (0, 2 * t[s] + h)),
                pl.BlockSpec((g, col), lambda s, t: (0, 2 * (2 * t[s] + t[8]) + h)),
            ],
            out_specs=[full] * 4,
        ),
        out_shape=outs,
    )(jt, weights, mass, wa, wb, p0, p1, ctf)


def shift(v, axis, size, d):
    return lax.ppermute(v, axis, [((i + d) % size, i) for i in range(size)])


def flip_y(v, bits):
    return lax.ppermute(v, ("yh", "yl"), [(i ^ bits, i) for i in range(4)])


def flip_core(v):
    return lax.ppermute(v, "core", [(0, 1), (1, 0)])


def f32(v):
    return v.astype(F32)


def shards(particles, projections, ctf, group_ids):
    n, f = particles.shape
    rows = projections.shape[0]
    nz = lax.axis_size("z")
    inverse = 4.0 / math.sqrt(f)
    pose_total = rows * nz * 2
    factor = pose_total / (n * 16 * 2 * nz)
    core = lax.axis_index("core")
    x = lax.axis_index("x")
    yh = lax.axis_index("yh")
    z = lax.axis_index("z")
    parity = core[None].astype(jnp.int32)
    ids = group_ids[None, :]

    nb = f // BLK // 2
    mine = lax.dynamic_slice(
        projections.reshape(rows, nb, 2, BLK), (0, 0, core, 0), (rows, nb, 1, BLK)
    ).reshape(rows, nb * BLK)
    hw = nb * BLK // 2

    near = {d: shift(mine, "z", nz, d) for d in (1, -1, 2, -2)}
    far = {d: shift(near[2 * d], "z", nz, d) for d in (1, -1)}
    opp_l = shift(near[2][:, :hw], "z", nz, 2)
    opp_r = shift(near[-2][:, hw:], "z", nz, -2)
    opp = jnp.concatenate([opp_l, opp_r], axis=1)

    first = [mine, near[1], near[2], near[-2], near[-1]]
    second = [far[1], opp, far[-1]]

    def other(blocks):
        stack = jnp.concatenate(blocks, axis=0)
        return flip_y(stack[:, :hw], 1), flip_y(stack[:, hw:], 3)

    f_l, f_r = other(first)
    s_l, s_r = other(second)

    def order(one, two):
        return jnp.concatenate([one[: 3 * rows], two, one[3 * rows :]], axis=0)

    proj_own = order(jnp.concatenate(first, axis=0), jnp.concatenate(second, axis=0))
    proj_oth = jnp.concatenate([order(f_l, s_l), order(f_r, s_r)], axis=1)

    w_send = weighted_call(1 - parity, ids, ctf, particles)
    w_recv = flip_core(w_send)
    w_own = weighted_call(parity, ids, ctf, particles)
    ids_all = jnp.concatenate([ids, flip_core(ids)], axis=1)

    s0, n0 = score_call(parity, w_own, w_recv, proj_own, ctf)
    s1, n1 = score_call(parity, w_own, w_recv, proj_oth, ctf)

    def swap(v):
        got = flip_core(v)
        return jnp.concatenate([got[n:], got[:n]], axis=0)

    r0, r1 = swap(s0), swap(s1)
    m0, m1 = flip_core(n0), flip_core(n1)
    log_norm, weights, mass = softmax_call(inverse, ids_all, (s0, r0, s1, r1, n0, m0, n1, m1))

    steps = jnp.arange(8, dtype=jnp.int32)
    jt = jnp.concatenate([(yh ^ (steps // 4)) * 4 + (x + steps) % 4, parity])
    args = (jt, weights, mass, w_own, w_recv, proj_own, proj_oth, ctf)
    ya = gradient_call(True, *args)
    xb = gradient_call(False, *args)

    ya_sum = ya[0] + f32(flip_y(ya[1], 1)) + f32(flip_y(ya[2], 2)) + f32(flip_y(ya[3], 3))
    xb_sum = xb[0]
    for d in (1, 2, 3):
        xb_sum = xb_sum + f32(shift(xb[d], "x", 4, -d))
    ya_two = ya_sum[0]
    for d in (1, 2, 3):
        ya_two = ya_two + f32(shift(ya_sum[d].astype(BF), "x", 4, -d))
    xb_two = xb_sum[0, 0]
    for a, b in ((0, 1), (1, 0), (1, 1)):
        xb_two = xb_two + f32(flip_y(xb_sum[a, b].astype(BF), 2 * a + b))
    both = jnp.concatenate([ya_two, xb_two], axis=1).astype(BF).reshape(nz, rows, BLK)
    both = lax.dynamic_slice(
        jnp.concatenate([both, both], axis=0), ((nz - z) % nz, 0, 0), (nz, rows, BLK)
    )
    parts = lax.all_to_all(both, "z", 0, 0)
    out = factor * jnp.sum(f32(parts), axis=0)
    return out, log_norm[:, 0]


def solution(mesh):
    fine = jax.sharding.Mesh(mesh.devices.reshape(2, 4, 2, 2, 8), NAMES)
    grp, pose = ("yh", "x", "core"), ("yl", "z")
    return jax.shard_map(
        shards,
        mesh=fine,
        in_specs=(P(grp + pose, None), P(pose, None), P(), P(grp + pose)),
        out_specs=(P(pose, grp), P(grp + pose)),
        check_vma=False,
    )
```

time: 301 us -> 147 us (0.49)
  waiting for transfers between devices: 246 us -> 34.4 us
  Pallas kernels: 0 us -> 56.4 us
  starting transfers between devices: 0.12 us -> 45.1 us
  matrix products: 40 us -> 0 us
  between operations: 13.9 us -> 1.01 us
  other arithmetic: 0.24 us -> 6.07 us
  local copies, waits for them, and re-layouts: 0.03 us -> 3.14 us
    reduce_scatter x2 -> x0, waiting for transfers between devices: 174 us -> none  [the longest x1 98.7 us: shards(): lax.psum_scatter(factor * numerator, 'pose', scatter_dimension=0, tiled=T...]
    all_gather x1 -> x0, waiting for transfers between devices: 72 us -> none  [shards(): gathered = lax.all_gather(projections, 'pose', axis=0, tiled=True)]
    pallas_call x0 -> x7, Pallas kernels: none -> 56.4 us  [the longest x2 19.2 us: score_call(): pl.pallas_call(score_kernel, grid_spec=pltpu.PrefetchScalarGridSpec(num_s...]
    ppermute x0 -> x30, starting transfers between devices: none -> 41.7 us  [the longest x14 24.7 us: shift(): return lax.ppermute(v, axis, [((i + d) % size, i) for i in range(size)])]
    dot_general x7 -> x0, matrix products: 40 us -> none  [the longest x1 10.2 us: shards(): jnp.dot(pose_mass, ctf_square, precision=high)]
    ppermute x0 -> x30, waiting for transfers between devices: none -> 26.1 us  [the longest x14 14.4 us: shift(): return lax.ppermute(v, axis, [((i + d) % size, i) for i in range(size)])]
    all_to_all x0 -> x1, waiting for transfers between devices: none -> 8.26 us  [shards(): parts = lax.all_to_all(both, 'z', 0, 0)]
    concatenate x0 -> x8, other arithmetic: none -> 4.41 us  [the longest x1 1.11 us: shards(): jnp.concatenate([both, both], axis=0)]
  transfers between devices with their start and end apart: 3 -> 31, of which waited for: 3 -> 12; matrix products, arithmetic and copies ran while one was open for 3% -> 4% of each run, Pallas kernels for 0% -> 31%
where the time goes in v1:
time: 147 us; the launch traced here: 146 us
  Pallas kernels  56.4 us (38%)
  starting transfers between devices  45.1 us (31%)
  waiting for transfers between devices  34.4 us (23%)
  other arithmetic  6.07 us (4%)
  local copies, waits for them, and re-layouts  3.14 us (2%)
    ppermute x14, starting transfers between devices, shift(): return lax.ppermute(v, axis, [((i + d) % size, i) for i in range(size)])  24.7 us
    pallas_call x2, Pallas kernels, score_call(): pl.pallas_call(score_kernel, grid_spec=pltpu.PrefetchScalarGridSpec(num_s...  19.2 us
    pallas_call x2, Pallas kernels, gradient_call(): pl.pallas_call(functools.partial(gradient_kernel, by_y), grid_spec=pltpu....  17.6 us
    pallas_call x2, Pallas kernels, weighted_call(): pl.pallas_call(weighted_kernel, grid_spec=pltpu.PrefetchScalarGridSpec(nu...  17 us
    ppermute x10, starting transfers between devices, flip_y(): return lax.ppermute(v, ('yh', 'yl'), [(i ^ bits, i) for i in range(4)])  15.9 us
    ppermute x14, waiting for transfers between devices, shift(): return lax.ppermute(v, axis, [((i + d) % size, i) for i in range(size)])  14.4 us
    ppermute x10, waiting for transfers between devices, flip_y(): return lax.ppermute(v, ('yh', 'yl'), [(i ^ bits, i) for i in range(4)])  10.8 us
    all_to_all x1, waiting for transfers between devices, shards(): parts = lax.all_to_all(both, 'z', 0, 0)  8.26 us
  transfers between devices with their start and end apart: 31, of which 12 were waited for; matrix products, arithmetic and copies ran while one was open for 4% of the time, Pallas kernels for 31%

profile of v1, /device:TPU:2, one launch (start us, length us, event | category | flops | bytes accessed | tf_op | source)
XLA Modules:
  0.0 146.1 jit_solution(12385996093894007201)
XLA Ops:
  0.6 0.0 copy-start
  0.7 0.9 copy-done
  1.6 5.9 %collective-permute-start.2 = (bf16[8,8192]{1,0:T(8,128)(2,1)S(1)}, bf16[8,8192]{1,0:T(8,128)(2,1)S(1)}, u32[]{:S(2)}, u32[]{:S(2)}) collective-permute-start(bf16[8,8192]{1,0:T(8,128)(2,1)S(1)} %bitcast.46), channel_id=1, source_target_pairs={{1,0},{2,1},{3,2},{4,3},{5,4},{6,5},{7,6},{0,7},{9,8},{10,9},{11,1... | collective-permute-start | bytes 393224 | tf_op jit(solution)/shard_map/ppermute | solution.py:215
  7.5 1.5 collective-permute-start.3
  9.0 1.5 %collective-permute-start.6 = (bf16[8,8192]{1,0:T(8,128)(2,1)S(1)}, bf16[8,8192]{1,0:T(8,128)(2,1)S(1)}, u32[]{:S(2)}, u32[]{:S(2)}) collective-permute-start(bf16[8,8192]{1,0:T(8,128)(2,1)S(1)} %bitcast.48), channel_id=1, source_target_pairs={{6,0},{7,1},{0,2},{1,3},{2,4},{3,5},{4,6},{5,7},{14,8},{15,9},{8,1... | collective-permute-start | bytes 393224 | tf_op jit(solution)/shard_map/ppermute | solution.py:215
  10.5 1.2 broadcast_in_dim.7.ids_ref
  11.7 8.5 %shard_map.60 = bf16[320,8192]{1,0:T(8,128)(2,1)} custom-call(s32[1]{0:T(128)S(6)} %sub.11.par_ref, s32[1,320]{1,0:T(1,128)} %broadcast_in_dim.7.ids_ref, bf16[32,16384]{1,0:T(8,128)(2,1)} %ctf_ref.11, bf16[320,16384]{1,0:T(8,128)(2,1)} %part_ref.3), custom_call_target="tpu_custom_call" | custom-call | tf_op jit(solution)/shard_map/pallas_call | solution.py:52
  20.2 3.8 %collective-permute-start.5 = (bf16[8,4096]{1,0:T(8,128)(2,1)S(1)}, bf16[8,4096]{1,0:T(8,128)(2,1)S(1)}, u32[]{:S(2)}, u32[]{:S(2)}) collective-permute-start(bf16[8,4096]{1,0:T(8,128)(2,1)S(1)} %slice.98), channel_id=1, source_target_pairs={{2,0},{3,1},{4,2},{5,3},{6,4},{7,5},{0,6},{1,7},{10,8},{11,9},{12,... | collective-permute-start | bytes 196616 | tf_op jit(solution)/shard_map/ppermute | solution.py:215
  24.0 0.1 collective-permute-start.7
  24.1 3.7 %collective-permute-start.4 = (bf16[8,8192]{1,0:T(8,128)(2,1)S(1)}, bf16[8,8192]{1,0:T(8,128)(2,1)S(1)}, u32[]{:S(2)}, u32[]{:S(2)}) collective-permute-start(bf16[8,8192]{1,0:T(8,128)(2,1)S(1)} %collective-permute-done.3), channel_id=1, source_target_pairs={{1,0},{2,1},{3,2},{4,3},{5,4},{6,5},{7,6},{0,7},{9,8},{10,9},{11,1... | collective-permute-start | bytes 393224 | tf_op jit(solution)/shard_map/ppermute | solution.py:215
  27.8 3.5 %collective-permute-done.4 = bf16[8,8192]{1,0:T(8,128)(2,1)S(1)} collective-permute-done((bf16[8,8192]{1,0:T(8,128)(2,1)S(1)}, bf16[8,8192]{1,0:T(8,128)(2,1)S(1)}, u32[]{:S(2)}, u32[]{:S(2)}) %collective-permute-start.4) | collective-permute-done | bytes 131104 | tf_op jit(solution)/shard_map/ppermute | solution.py:215
  31.3 0.0 collective-permute-start.8
  31.4 0.4 collective-permute-done.7
  31.8 6.3 %collective-permute-done.8 = bf16[8,8192]{1,0:T(8,128)(2,1)S(1)} collective-permute-done((bf16[8,8192]{1,0:T(8,128)(2,1)S(1)}, bf16[8,8192]{1,0:T(8,128)(2,1)S(1)}, u32[]{:S(2)}, u32[]{:S(2)}) %collective-permute-start.8) | collective-permute-done | bytes 131104 | tf_op jit(solution)/shard_map/ppermute | solution.py:215
  38.2 1.7 %collective-permute-start.11 = (bf16[40,4096]{1,0:T(8,128)(2,1)S(1)}, bf16[40,4096]{1,0:T(8,128)(2,1)S(1)}, u32[]{:S(2)}, u32[]{:S(2)}) collective-permute-start(bf16[40,4096]{1,0:T(8,128)(2,1)S(1)} %get-tuple-element.36), channel_id=1, source_target_pairs={{8,0},{0,8},{136,128},{128,136},{9,1},{1,9},{137,129},{129,137},{1... | collective-permute-start | bytes 983048 | tf_op jit(solution)/shard_map/ppermute | solution.py:219
  39.8 2.2 %collective-permute-start.13 = (bf16[40,4096]{1,0:T(8,128)(2,1)S(1)}, bf16[40,4096]{1,0:T(8,128)(2,1)S(1)}, u32[]{:S(2)}, u32[]{:S(2)}) collective-permute-start(bf16[40,4096]{1,0:T(8,128)(2,1)S(1)} %get-tuple-element.37), channel_id=1, source_target_pairs={{136,0},{128,8},{8,128},{0,136},{137,1},{129,9},{9,129},{1,137},{1... | collective-permute-start | bytes 983048 | tf_op jit(solution)/shard_map/ppermute | solution.py:219
  42.1 0.7 collective-permute-start.12
  42.8 0.6 collective-permute-start.14
  43.4 8.5 %shard_map.59.wa_ref = bf16[320,8192]{1,0:T(8,128)(2,1)} custom-call(s32[1]{0:T(128)} %bitcast.par_ref, s32[1,320]{1,0:T(1,128)} %broadcast_in_dim.7.ids_ref, bf16[32,16384]{1,0:T(8,128)(2,1)} %ctf_ref.11, bf16[320,16384]{1,0:T(8,128)(2,1)} %part_ref.3), custom_call_target="tpu_custom_call" | custom-call | tf_op jit(solution)/shard_map/pallas_call | solution.py:52
  52.0 0.0 collective-permute-done.11
  52.0 0.1 collective-permute-start
  52.1 0.0 collective-permute-done.13
  52.2 0.0 collective-permute-done.12
  52.2 1.6 %collective-permute-done.14 = bf16[24,4096]{1,0:T(8,128)(2,1)S(1)} collective-permute-done((bf16[24,4096]{1,0:T(8,128)(2,1)S(1)}, bf16[24,4096]{1,0:T(8,128)(2,1)S(1)}, u32[]{:S(2)}, u32[]{:S(2)}) %collective-permute-start.14) | collective-permute-done | bytes 196640 | tf_op jit(solution)/shard_map/ppermute | solution.py:219
  53.8 1.1 maximum_maximum_fusion.proj_ref.p1_ref
  54.9 9.6 %shard_map.62 = (f32[640,64]{1,0:T(8,128)}, f32[32,64]{1,0:T(8,128)}) custom-call(s32[1]{0:T(128)} %bitcast.par_ref, bf16[320,8192]{1,0:T(8,128)(2,1)} %shard_map.59.wa_ref, bf16[320,8192]{1,0:T(8,128)(2,1)} %collective-permute-done.1.wb_ref, bf16[64,8192]{1,0:T(8,128)(2,1)} %maximum_maximum_fusion.proj_ref.p1_ref, bf16[32,16384]{1,0:T(8,128)(2,1)} %ctf_ref.11), custom_call_target="tpu_custom_call" | custom-call | tf_op jit(solution)/shard_map/pallas_call | solution.py:100
  64.5 0.6 pad_add_fusion.1.jt_ref
  65.1 0.6 pad_add_fusion.ids_ref
  65.7 9.6 %shard_map.61 = (f32[640,64]{1,0:T(8,128)}, f32[32,64]{1,0:T(8,128)}) custom-call(s32[1]{0:T(128)} %bitcast.par_ref, bf16[320,8192]{1,0:T(8,128)(2,1)} %shard_map.59.wa_ref, bf16[320,8192]{1,0:T(8,128)(2,1)} %collective-permute-done.1.wb_ref, bf16[64,8192]{1,0:T(8,128)(2,1)} %copy-done.1, bf16[32,16384]{1,0:T(8,128)(2,1)} %ctf_ref.11), custom_call_target="tpu_custom_call" | custom-call | tf_op jit(solution)/shard_map/pallas_call | solution.py:100
  75.4 0.5 collective-permute-start.10
  75.9 0.1 collective-permute-start.17
  76.0 0.4 collective-permute-start.16
  76.4 0.0 collective-permute-done.15
  76.4 0.9 collective-permute-done.10
  77.4 0.9 pad_maximum_fusion.1
  78.3 0.6 copy-done.7
  78.9 0.0 copy-done.8
  78.9 2.7 %shard_map.63 = (f32[320,1]{1,0:T(8,128)}, bf16[640,128]{1,0:T(8,128)(2,1)}, f32[32,128]{1,0:T(8,128)}) custom-call(s32[1,640]{1,0:T(1,128)} %pad_add_fusion.ids_ref, f32[640,64]{1,0:T(8,128)} %get-tuple-element.17.refs_0_, f32[640,64]{1,0:T(8,128)} %get-tuple-element.60.refs_1_, f32[640,64]{1,0:T(8,128)} %get-tuple-element.18.refs_2_, ...), custom_call_target="tpu_custom_call" | custom-call | tf_op jit(solution)/shard_map/pallas_call | solution.py:143
  81.5 8.8 %shard_map.65 = (f32[2,2,64,512]{3,2,1,0:T(8,128)}, bf16[2,2,64,512]{3,2,1,0:T(8,128)(2,1)}, bf16[2,2,64,512]{3,2,1,0:T(8,128)(2,1)}, bf16[2,2,64,512]{3,2,1,0:T(8,128)(2,1)}) custom-call(s32[9]{0:T(128)} %pad_add_fusion.1.jt_ref, bf16[640,128]{1,0:T(8,128)(2,1)} %get-tuple-element.21.w_ref, f32[32,128]{1,0:T(8,128)} %get-tuple-element.22.mass_ref, ...), custom_call_target="tpu_custom_call" | custom-call | tf_op jit(solution)/shard_map/pallas_call | solution.py:194
  90.3 1.5 %collective-permute-start.24 = (bf16[2,2,64,512]{3,2,1,0:T(8,128)(2,1)}, bf16[2,2,64,512]{3,2,1,0:T(8,128)(2,1)S(1)}, u32[]{:S(2)}, u32[]{:S(2)}) collective-permute-start(bf16[2,2,64,512]{3,2,1,0:T(8,128)(2,1)} %get-tuple-element.28), channel_id=1, source_target_pairs={{96,0},{0,32},{32,64},{64,96},{97,1},{1,33},{33,65},{65,97},{98,2}... | collective-permute-start | bytes 786440 | tf_op jit(solution)/shard_map/ppermute | solution.py:215
  91.8 1.1 collective-permute-start.25
  92.9 2.2 %collective-permute-start.26 = (bf16[2,2,64,512]{3,2,1,0:T(8,128)(2,1)}, bf16[2,2,64,512]{3,2,1,0:T(8,128)(2,1)S(1)}, u32[]{:S(2)}, u32[]{:S(2)}) collective-permute-start(bf16[2,2,64,512]{3,2,1,0:T(8,128)(2,1)} %get-tuple-element.30), channel_id=1, source_target_pairs={{32,0},{64,32},{96,64},{0,96},{33,1},{65,33},{97,65},{1,97},{34,2}... | collective-permute-start | bytes 786440 | tf_op jit(solution)/shard_map/ppermute | solution.py:215
  95.1 8.8 %shard_map.64 = (f32[4,64,512]{2,1,0:T(8,128)}, bf16[4,64,512]{2,1,0:T(8,128)(2,1)}, bf16[4,64,512]{2,1,0:T(8,128)(2,1)}, bf16[4,64,512]{2,1,0:T(8,128)(2,1)}) custom-call(s32[9]{0:T(128)} %pad_add_fusion.1.jt_ref, bf16[640,128]{1,0:T(8,128)(2,1)} %get-tuple-element.21.w_ref, f32[32,128]{1,0:T(8,128)} %get-tuple-element.22.mass_ref, ...), custom_call_target="tpu_custom_call" | custom-call | tf_op jit(solution)/shard_map/pallas_call | solution.py:194
  103.9 0.1 collective-permute-start.18
  103.9 3.6 %collective-permute-start.19 = (bf16[4,64,512]{2,1,0:T(8,128)(2,1)}, bf16[4,64,512]{2,1,0:T(8,128)(2,1)S(1)}, u32[]{:S(2)}, u32[]{:S(2)}) collective-permute-start(bf16[4,64,512]{2,1,0:T(8,128)(2,1)} %get-tuple-element.25), channel_id=1, source_target_pairs={{128,0},{136,8},{0,128},{8,136},{129,1},{137,9},{1,129},{9,137},{1... | collective-permute-start | bytes 786440 | tf_op jit(solution)/shard_map/ppermute | solution.py:219
  107.6 1.1 collective-permute-start.20
  108.6 0.1 fusion.19
  108.8 0.1 collective-permute-start.27
  108.9 3.6 %collective-permute-start.28 = (bf16[64,512]{1,0:T(8,128)(2,1)S(1)}, bf16[64,512]{1,0:T(8,128)(2,1)S(1)}, u32[]{:S(2)}, u32[]{:S(2)}) collective-permute-start(bf16[64,512]{1,0:T(8,128)(2,1)S(1)} %get-tuple-element.46), channel_id=1, source_target_pairs={{128,0},{136,8},{0,128},{8,136},{129,1},{137,9},{1,129},{9,137},{1... | collective-permute-start | bytes 196616 | tf_op jit(solution)/shard_map/ppermute | solution.py:219
  112.6 0.8 collective-permute-done.18
  113.4 2.2 %collective-permute-start.29 = (bf16[64,512]{1,0:T(8,128)(2,1)S(1)}, bf16[64,512]{1,0:T(8,128)(2,1)S(1)}, u32[]{:S(2)}, u32[]{:S(2)}) collective-permute-start(bf16[64,512]{1,0:T(8,128)(2,1)S(1)} %get-tuple-element.45), channel_id=1, source_target_pairs={{136,0},{128,8},{8,128},{0,136},{137,1},{129,9},{9,129},{1,137},{1... | collective-permute-start | bytes 196616 | tf_op jit(solution)/shard_map/ppermute | solution.py:219
  115.6 5.1 %collective-permute-done.19 = bf16[4,64,512]{2,1,0:T(8,128)(2,1)S(1)} collective-permute-done((bf16[4,64,512]{2,1,0:T(8,128)(2,1)}, bf16[4,64,512]{2,1,0:T(8,128)(2,1)S(1)}, u32[]{:S(2)}, u32[]{:S(2)}) %collective-permute-start.19) | collective-permute-done | bytes 262176 | tf_op jit(solution)/shard_map/ppermute | solution.py:219
  120.6 3.3 %collective-permute-done.20 = bf16[4,64,512]{2,1,0:T(8,128)(2,1)S(1)} collective-permute-done((bf16[4,64,512]{2,1,0:T(8,128)(2,1)}, bf16[4,64,512]{2,1,0:T(8,128)(2,1)S(1)}, u32[]{:S(2)}, u32[]{:S(2)}) %collective-permute-start.20) | collective-permute-done | bytes 262176 | tf_op jit(solution)/shard_map/ppermute | solution.py:219
  123.9 0.1 fusion.20
  124.1 0.1 collective-permute-start.21
  124.2 3.5 %collective-permute-start.22 = (bf16[64,512]{1,0:T(8,128)(2,1)S(1)}, bf16[64,512]{1,0:T(8,128)(2,1)S(1)}, u32[]{:S(2)}, u32[]{:S(2)}) collective-permute-start(bf16[64,512]{1,0:T(8,128)(2,1)S(1)} %get-tuple-element.49), channel_id=1, source_target_pairs={{64,0},{96,32},{0,64},{32,96},{65,1},{97,33},{1,65},{33,97},{66,2}... | collective-permute-start | bytes 196616 | tf_op jit(solution)/shard_map/ppermute | solution.py:215
  127.7 0.7 collective-permute-done.21
  128.4 1.6 %collective-permute-done.22 = bf16[64,512]{1,0:T(8,128)(2,1)S(1)} collective-permute-done((bf16[64,512]{1,0:T(8,128)(2,1)S(1)}, bf16[64,512]{1,0:T(8,128)(2,1)S(1)}, u32[]{:S(2)}, u32[]{:S(2)}) %collective-permute-start.22) | collective-permute-done | bytes 65568 | tf_op jit(solution)/shard_map/ppermute | solution.py:215
  130.0 1.9 %collective-permute-done.23 = bf16[64,512]{1,0:T(8,128)(2,1)S(1)} collective-permute-done((bf16[64,512]{1,0:T(8,128)(2,1)S(1)}, bf16[64,512]{1,0:T(8,128)(2,1)S(1)}, u32[]{:S(2)}, u32[]{:S(2)}) %collective-permute-start.23) | collective-permute-done | bytes 65568 | tf_op jit(solution)/shard_map/ppermute | solution.py:215
  132.0 1.1 fusion.3
  133.1 3.4 %all-to-all-start = ((bf16[8,8,1024]{2,1,0:T(8,128)(2,1)}), bf16[8,8,1024]{2,1,0:T(8,128)(2,1)S(1)}, u32[]{:S(2)}, u32[]{:S(2)}) async-start(bf16[8,8,1024]{2,1,0:T(8,128)(2,1)} %fusion.3), calls=%async_computation | async-start | bytes 262144 | tf_op jit(solution)/shard_map/all_to_all | solution.py:308
  136.5 0.7 reduce
  137.2 8.3 %all-to-all-done = bf16[8,8,1024]{2,1,0:T(8,128)(2,1)S(1)} async-done(((bf16[8,8,1024]{2,1,0:T(8,128)(2,1)}), bf16[8,8,1024]{2,1,0:T(8,128)(2,1)S(1)}, u32[]{:S(2)}, u32[]{:S(2)}) %all-to-all-start) | async-done | bytes 131104 | tf_op jit(solution)/shard_map/all_to_all | solution.py:308
  145.5 0.6 broadcast_multiply_fusion
  (60 shorter events, 0.5 us)
Async XLA Ops:
  0.6 1.0 copy-start
  1.6 22.5 %collective-permute-start.2 = (bf16[8,8192]{1,0:T(8,128)(2,1)S(1)}, bf16[8,8192]{1,0:T(8,128)(2,1)S(1)}, u32[]{:S(2)}, u32[]{:S(2)}) collective-permute-start(bf16[8,8192]{1,0:T(8,128)(2,1)S(1)} %bitcast.46), channel_id=1, source_target_pairs={{1,0},{2,1},{3,2},{4,3},{5,4},{6,5},{7,6},{0,7},{9,8},{10,9},{11,1... | collective-permute-start | bytes 393224 | tf_op jit(solution)/shard_map/ppermute | solution.py:215
  7.5 12.7 %collective-permute-start.3 = (bf16[8,8192]{1,0:T(8,128)(2,1)S(1)}, bf16[8,8192]{1,0:T(8,128)(2,1)S(1)}, u32[]{:S(2)}, u32[]{:S(2)}) collective-permute-start(bf16[8,8192]{1,0:T(8,128)(2,1)S(1)} %bitcast.47), channel_id=1, source_target_pairs={{2,0},{3,1},{4,2},{5,3},{6,4},{7,5},{0,6},{1,7},{10,8},{11,9},{12,... | collective-permute-start | bytes 393224 | tf_op jit(solution)/shard_map/ppermute | solution.py:215
  9.0 15.0 %collective-permute-start.6 = (bf16[8,8192]{1,0:T(8,128)(2,1)S(1)}, bf16[8,8192]{1,0:T(8,128)(2,1)S(1)}, u32[]{:S(2)}, u32[]{:S(2)}) collective-permute-start(bf16[8,8192]{1,0:T(8,128)(2,1)S(1)} %bitcast.48), channel_id=1, source_target_pairs={{6,0},{7,1},{0,2},{1,3},{2,4},{3,5},{4,6},{5,7},{14,8},{15,9},{8,1... | collective-permute-start | bytes 393224 | tf_op jit(solution)/shard_map/ppermute | solution.py:215
  10.5 27.6 %collective-permute-start.9 = (bf16[8,8192]{1,0:T(8,128)(2,1)S(1)}, bf16[8,8192]{1,0:T(8,128)(2,1)S(1)}, u32[]{:S(2)}, u32[]{:S(2)}) collective-permute-start(bf16[8,8192]{1,0:T(8,128)(2,1)S(1)} %bitcast.49), channel_id=1, source_target_pairs={{7,0},{0,1},{1,2},{2,3},{3,4},{4,5},{5,6},{6,7},{15,8},{8,9},{9,10... | collective-permute-start | bytes 393224 | tf_op jit(solution)/shard_map/ppermute | solution.py:215
  20.2 34.7 %collective-permute-start.1 = (bf16[320,8192]{1,0:T(8,128)(2,1)}, bf16[320,8192]{1,0:T(8,128)(2,1)}, u32[]{:S(2)}, u32[]{:S(2)}) collective-permute-start(bf16[320,8192]{1,0:T(8,128)(2,1)} %shard_map.60), channel_id=1, source_target_pairs={{0,16},{16,0},{1,17},{17,1},{2,18},{18,2},{3,19},{19,3},{4,20},{20... | collective-permute-start | bytes 15728648 | tf_op jit(solution)/shard_map/ppermute | solution.py:223
  20.2 11.1 %collective-permute-start.5 = (bf16[8,4096]{1,0:T(8,128)(2,1)S(1)}, bf16[8,4096]{1,0:T(8,128)(2,1)S(1)}, u32[]{:S(2)}, u32[]{:S(2)}) collective-permute-start(bf16[8,4096]{1,0:T(8,128)(2,1)S(1)} %slice.98), channel_id=1, source_target_pairs={{2,0},{3,1},{4,2},{5,3},{6,4},{7,5},{0,6},{1,7},{10,8},{11,9},{12,... | collective-permute-start | bytes 196616 | tf_op jit(solution)/shard_map/ppermute | solution.py:215
  24.0 7.7 %collective-permute-start.7 = (bf16[8,4096]{1,0:T(8,128)(2,1)S(1)}, bf16[8,4096]{1,0:T(8,128)(2,1)S(1)}, u32[]{:S(2)}, u32[]{:S(2)}) collective-permute-start(bf16[8,4096]{1,0:T(8,128)(2,1)S(1)} %slice.99), channel_id=1, source_target_pairs={{6,0},{7,1},{0,2},{1,3},{2,4},{3,5},{4,6},{5,7},{14,8},{15,9},{8,1... | collective-permute-start | bytes 196616 | tf_op jit(solution)/shard_map/ppermute | solution.py:215
  24.1 7.2 %collective-permute-start.4 = (bf16[8,8192]{1,0:T(8,128)(2,1)S(1)}, bf16[8,8192]{1,0:T(8,128)(2,1)S(1)}, u32[]{:S(2)}, u32[]{:S(2)}) collective-permute-start(bf16[8,8192]{1,0:T(8,128)(2,1)S(1)} %collective-permute-done.3), channel_id=1, source_target_pairs={{1,0},{2,1},{3,2},{4,3},{5,4},{6,5},{7,6},{0,7},{9,8},{10,9},{11,1... | collective-permute-start | bytes 393224 | tf_op jit(solution)/shard_map/ppermute | solution.py:215
  31.3 6.7 %collective-permute-start.8 = (bf16[8,8192]{1,0:T(8,128)(2,1)S(1)}, bf16[8,8192]{1,0:T(8,128)(2,1)S(1)}, u32[]{:S(2)}, u32[]{:S(2)}) collective-permute-start(bf16[8,8192]{1,0:T(8,128)(2,1)S(1)} %collective-permute-done.6), channel_id=1, source_target_pairs={{7,0},{0,1},{1,2},{2,3},{3,4},{4,5},{5,6},{6,7},{15,8},{8,9},{9,10... | collective-permute-start | bytes 393224 | tf_op jit(solution)/shard_map/ppermute | solution.py:215
  38.1 13.9 %copy-start.1 = (bf16[64,8192]{1,0:T(8,128)(2,1)}, bf16[64,8192]{1,0:T(8,128)(2,1)S(1)}, u32[]{:S(2)}) copy-start(bf16[64,8192]{1,0:T(8,128)(2,1)S(1)} %get-tuple-element.51.proj_ref.p0_ref) | copy-start | bytes 3145732
  38.2 13.8 %collective-permute-start.11 = (bf16[40,4096]{1,0:T(8,128)(2,1)S(1)}, bf16[40,4096]{1,0:T(8,128)(2,1)S(1)}, u32[]{:S(2)}, u32[]{:S(2)}) collective-permute-start(bf16[40,4096]{1,0:T(8,128)(2,1)S(1)} %get-tuple-element.36), channel_id=1, source_target_pairs={{8,0},{0,8},{136,128},{128,136},{9,1},{1,9},{137,129},{129,137},{1... | collective-permute-start | bytes 983048 | tf_op jit(solution)/shard_map/ppermute | solution.py:219
  39.8 12.3 %collective-permute-start.13 = (bf16[40,4096]{1,0:T(8,128)(2,1)S(1)}, bf16[40,4096]{1,0:T(8,128)(2,1)S(1)}, u32[]{:S(2)}, u32[]{:S(2)}) collective-permute-start(bf16[40,4096]{1,0:T(8,128)(2,1)S(1)} %get-tuple-element.37), channel_id=1, source_target_pairs={{136,0},{128,8},{8,128},{0,136},{137,1},{129,9},{9,129},{1,137},{1... | collective-permute-start | bytes 983048 | tf_op jit(solution)/shard_map/ppermute | solution.py:219
  42.1 10.1 %collective-permute-start.12 = (bf16[24,4096]{1,0:T(8,128)(2,1)S(1)}, bf16[24,4096]{1,0:T(8,128)(2,1)S(1)}, u32[]{:S(2)}, u32[]{:S(2)}) collective-permute-start(bf16[24,4096]{1,0:T(8,128)(2,1)S(1)} %get-tuple-element.38), channel_id=1, source_target_pairs={{8,0},{0,8},{136,128},{128,136},{9,1},{1,9},{137,129},{129,137},{1... | collective-permute-start | bytes 589832 | tf_op jit(solution)/shard_map/ppermute | solution.py:219
  42.8 9.1 %copy-start.5 = (s32[1,320]{1,0:T(1,128)S(1)}, s32[1,320]{1,0:T(1,128)}, u32[]{:S(2)}) copy-start(s32[1,320]{1,0:T(1,128)} %broadcast_in_dim.7.ids_ref) | copy-start | bytes 3844
  42.8 11.0 %collective-permute-start.14 = (bf16[24,4096]{1,0:T(8,128)(2,1)S(1)}, bf16[24,4096]{1,0:T(8,128)(2,1)S(1)}, u32[]{:S(2)}, u32[]{:S(2)}) collective-permute-start(bf16[24,4096]{1,0:T(8,128)(2,1)S(1)} %get-tuple-element.39), channel_id=1, source_target_pairs={{136,0},{128,8},{8,128},{0,136},{137,1},{129,9},{9,129},{1,137},{1... | collective-permute-start | bytes 589832 | tf_op jit(solution)/shard_map/ppermute | solution.py:219
  52.0 13.1 %collective-permute-start = (s32[1,320]{1,0:T(1,128)S(1)}, s32[1,320]{1,0:T(1,128)S(1)}, u32[]{:S(2)}, u32[]{:S(2)}) collective-permute-start(s32[1,320]{1,0:T(1,128)S(1)} %copy-done.5), channel_id=1, source_target_pairs={{0,16},{16,0},{1,17},{17,1},{2,18},{18,2},{3,19},{19,3},{4,20},{20... | collective-permute-start | bytes 3848 | tf_op jit(solution)/shard_map/ppermute | solution.py:223
  64.5 11.9 %collective-permute-start.15 = (f32[640,64]{1,0:T(8,128)}, f32[640,64]{1,0:T(8,128)S(1)}, u32[]{:S(2)}, u32[]{:S(2)}) collective-permute-start(f32[640,64]{1,0:T(8,128)} %get-tuple-element.18.refs_2_), channel_id=1, source_target_pairs={{0,16},{16,0},{1,17},{17,1},{2,18},{18,2},{3,19},{19,3},{4,20},{20... | collective-permute-start | bytes 491528 | tf_op jit(solution)/shard_map/ppermute | solution.py:223
  65.7 10.1 %copy-start.6 = (f32[32,64]{1,0:T(8,128)S(1)}, f32[32,64]{1,0:T(8,128)}, u32[]{:S(2)}) copy-start(f32[32,64]{1,0:T(8,128)} %get-tuple-element.20.refs_6_) | copy-start | bytes 24580
  75.4 2.0 %collective-permute-start.10 = (f32[640,64]{1,0:T(8,128)}, f32[640,64]{1,0:T(8,128)S(1)}, u32[]{:S(2)}, u32[]{:S(2)}) collective-permute-start(f32[640,64]{1,0:T(8,128)} %get-tuple-element.17.refs_0_), channel_id=1, source_target_pairs={{0,16},{16,0},{1,17},{17,1},{2,18},{18,2},{3,19},{19,3},{4,20},{20... | collective-permute-start | bytes 491528 | tf_op jit(solution)/shard_map/ppermute | solution.py:223
  75.9 2.4 %collective-permute-start.17 = (f32[32,64]{1,0:T(8,128)S(1)}, f32[32,64]{1,0:T(8,128)S(1)}, u32[]{:S(2)}, u32[]{:S(2)}) collective-permute-start(f32[32,64]{1,0:T(8,128)S(1)} %copy-done.6), channel_id=1, source_target_pairs={{0,16},{16,0},{1,17},{17,1},{2,18},{18,2},{3,19},{19,3},{4,20},{20... | collective-permute-start | bytes 24584 | tf_op jit(solution)/shard_map/ppermute | solution.py:223
  76.0 2.3 %collective-permute-start.16 = (f32[32,64]{1,0:T(8,128)}, f32[32,64]{1,0:T(8,128)S(1)}, u32[]{:S(2)}, u32[]{:S(2)}) collective-permute-start(f32[32,64]{1,0:T(8,128)} %get-tuple-element.19.refs_4_), channel_id=1, source_target_pairs={{0,16},{16,0},{1,17},{17,1},{2,18},{18,2},{3,19},{19,3},{4,20},{20... | collective-permute-start | bytes 24584 | tf_op jit(solution)/shard_map/ppermute | solution.py:223
  78.3 0.6 copy-start.7
  78.3 0.6 copy-start.8
  90.3 17.3 %collective-permute-start.24 = (bf16[2,2,64,512]{3,2,1,0:T(8,128)(2,1)}, bf16[2,2,64,512]{3,2,1,0:T(8,128)(2,1)S(1)}, u32[]{:S(2)}, u32[]{:S(2)}) collective-permute-start(bf16[2,2,64,512]{3,2,1,0:T(8,128)(2,1)} %get-tuple-element.28), channel_id=1, source_target_pairs={{96,0},{0,32},{32,64},{64,96},{97,1},{1,33},{33,65},{65,97},{98,2}... | collective-permute-start | bytes 786440 | tf_op jit(solution)/shard_map/ppermute | solution.py:215
  91.8 16.8 %collective-permute-start.25 = (bf16[2,2,64,512]{3,2,1,0:T(8,128)(2,1)}, bf16[2,2,64,512]{3,2,1,0:T(8,128)(2,1)S(1)}, u32[]{:S(2)}, u32[]{:S(2)}) collective-permute-start(bf16[2,2,64,512]{3,2,1,0:T(8,128)(2,1)} %get-tuple-element.29), channel_id=1, source_target_pairs={{64,0},{96,32},{0,64},{32,96},{65,1},{97,33},{1,65},{33,97},{66,2}... | collective-permute-start | bytes 786440 | tf_op jit(solution)/shard_map/ppermute | solution.py:215
  92.9 15.7 %collective-permute-start.26 = (bf16[2,2,64,512]{3,2,1,0:T(8,128)(2,1)}, bf16[2,2,64,512]{3,2,1,0:T(8,128)(2,1)S(1)}, u32[]{:S(2)}, u32[]{:S(2)}) collective-permute-start(bf16[2,2,64,512]{3,2,1,0:T(8,128)(2,1)} %get-tuple-element.30), channel_id=1, source_target_pairs={{32,0},{64,32},{96,64},{0,96},{33,1},{65,33},{97,65},{1,97},{34,2}... | collective-permute-start | bytes 786440 | tf_op jit(solution)/shard_map/ppermute | solution.py:215
  95.1 13.6 %copy-start.2 = (f32[2,2,64,512]{3,2,1,0:T(8,128)S(1)}, f32[2,2,64,512]{3,2,1,0:T(8,128)}, u32[]{:S(2)}) copy-start(f32[2,2,64,512]{3,2,1,0:T(8,128)} %get-tuple-element.27) | copy-start | bytes 1572868
  103.9 20.0 %copy-start.3 = (f32[4,64,512]{2,1,0:T(8,128)S(1)}, f32[4,64,512]{2,1,0:T(8,128)}, u32[]{:S(2)}) copy-start(f32[4,64,512]{2,1,0:T(8,128)} %get-tuple-element.23) | copy-start | bytes 1572868
  103.9 9.5 %collective-permute-start.18 = (bf16[4,64,512]{2,1,0:T(8,128)(2,1)}, bf16[4,64,512]{2,1,0:T(8,128)(2,1)S(1)}, u32[]{:S(2)}, u32[]{:S(2)}) collective-permute-start(bf16[4,64,512]{2,1,0:T(8,128)(2,1)} %get-tuple-element.24), channel_id=1, source_target_pairs={{8,0},{0,8},{136,128},{128,136},{9,1},{1,9},{137,129},{129,137},{1... | collective-permute-start | bytes 786440 | tf_op jit(solution)/shard_map/ppermute | solution.py:219
  103.9 16.7 %collective-permute-start.19 = (bf16[4,64,512]{2,1,0:T(8,128)(2,1)}, bf16[4,64,512]{2,1,0:T(8,128)(2,1)S(1)}, u32[]{:S(2)}, u32[]{:S(2)}) collective-permute-start(bf16[4,64,512]{2,1,0:T(8,128)(2,1)} %get-tuple-element.25), channel_id=1, source_target_pairs={{128,0},{136,8},{0,128},{8,136},{129,1},{137,9},{1,129},{9,137},{1... | collective-permute-start | bytes 786440 | tf_op jit(solution)/shard_map/ppermute | solution.py:219
  107.6 16.3 %collective-permute-start.20 = (bf16[4,64,512]{2,1,0:T(8,128)(2,1)}, bf16[4,64,512]{2,1,0:T(8,128)(2,1)S(1)}, u32[]{:S(2)}, u32[]{:S(2)}) collective-permute-start(bf16[4,64,512]{2,1,0:T(8,128)(2,1)} %get-tuple-element.26), channel_id=1, source_target_pairs={{136,0},{128,8},{8,128},{0,136},{137,1},{129,9},{9,129},{1,137},{1... | collective-permute-start | bytes 786440 | tf_op jit(solution)/shard_map/ppermute | solution.py:219
  108.8 27.7 %copy-start.4 = (f32[320,1]{1,0:T(8,128)S(1)}, f32[320,1]{1,0:T(8,128)}, u32[]{:S(2)}) copy-start(f32[320,1]{1,0:T(8,128)} %get-tuple-element.31) | copy-start | bytes 3844
  108.8 18.9 %collective-permute-start.27 = (bf16[64,512]{1,0:T(8,128)(2,1)S(1)}, bf16[64,512]{1,0:T(8,128)(2,1)S(1)}, u32[]{:S(2)}, u32[]{:S(2)}) collective-permute-start(bf16[64,512]{1,0:T(8,128)(2,1)S(1)} %get-tuple-element.44), channel_id=1, source_target_pairs={{8,0},{0,8},{136,128},{128,136},{9,1},{1,9},{137,129},{129,137},{1... | collective-permute-start | bytes 196616 | tf_op jit(solution)/shard_map/ppermute | solution.py:219
  108.9 18.8 %collective-permute-start.28 = (bf16[64,512]{1,0:T(8,128)(2,1)S(1)}, bf16[64,512]{1,0:T(8,128)(2,1)S(1)}, u32[]{:S(2)}, u32[]{:S(2)}) collective-permute-start(bf16[64,512]{1,0:T(8,128)(2,1)S(1)} %get-tuple-element.46), channel_id=1, source_target_pairs={{128,0},{136,8},{0,128},{8,136},{129,1},{137,9},{1,129},{9,137},{1... | collective-permute-start | bytes 196616 | tf_op jit(solution)/shard_map/ppermute | solution.py:219
  113.4 14.3 %collective-permute-start.29 = (bf16[64,512]{1,0:T(8,128)(2,1)S(1)}, bf16[64,512]{1,0:T(8,128)(2,1)S(1)}, u32[]{:S(2)}, u32[]{:S(2)}) collective-permute-start(bf16[64,512]{1,0:T(8,128)(2,1)S(1)} %get-tuple-element.45), channel_id=1, source_target_pairs={{136,0},{128,8},{8,128},{0,136},{137,1},{129,9},{9,129},{1,137},{1... | collective-permute-start | bytes 196616 | tf_op jit(solution)/shard_map/ppermute | solution.py:219
  124.1 4.3 %collective-permute-start.21 = (bf16[64,512]{1,0:T(8,128)(2,1)S(1)}, bf16[64,512]{1,0:T(8,128)(2,1)S(1)}, u32[]{:S(2)}, u32[]{:S(2)}) collective-permute-start(bf16[64,512]{1,0:T(8,128)(2,1)S(1)} %get-tuple-element.47), channel_id=1, source_target_pairs={{96,0},{0,32},{32,64},{64,96},{97,1},{1,33},{33,65},{65,97},{98,2}... | collective-permute-start | bytes 196616 | tf_op jit(solution)/shard_map/ppermute | solution.py:215
  124.2 5.9 %collective-permute-start.22 = (bf16[64,512]{1,0:T(8,128)(2,1)S(1)}, bf16[64,512]{1,0:T(8,128)(2,1)S(1)}, u32[]{:S(2)}, u32[]{:S(2)}) collective-permute-start(bf16[64,512]{1,0:T(8,128)(2,1)S(1)} %get-tuple-element.49), channel_id=1, source_target_pairs={{64,0},{96,32},{0,64},{32,96},{65,1},{97,33},{1,65},{33,97},{66,2}... | collective-permute-start | bytes 196616 | tf_op jit(solution)/shard_map/ppermute | solution.py:215
  127.7 4.3 %collective-permute-start.23 = (bf16[64,512]{1,0:T(8,128)(2,1)S(1)}, bf16[64,512]{1,0:T(8,128)(2,1)S(1)}, u32[]{:S(2)}, u32[]{:S(2)}) collective-permute-start(bf16[64,512]{1,0:T(8,128)(2,1)S(1)} %get-tuple-element.48), channel_id=1, source_target_pairs={{32,0},{64,32},{96,64},{0,96},{33,1},{65,33},{97,65},{1,97},{34,2}... | collective-permute-start | bytes 196616 | tf_op jit(solution)/shard_map/ppermute | solution.py:215
  133.1 12.4 %all-to-all-start = ((bf16[8,8,1024]{2,1,0:T(8,128)(2,1)}), bf16[8,8,1024]{2,1,0:T(8,128)(2,1)S(1)}, u32[]{:S(2)}, u32[]{:S(2)}) async-start(bf16[8,8,1024]{2,1,0:T(8,128)(2,1)} %fusion.3), calls=%async_computation | async-start | bytes 262144 | tf_op jit(solution)/shard_map/all_to_all | solution.py:308

commit v2 on v0

v2 whole, which is shorter than its diff:
```python
import functools
import math

import jax
import jax.numpy as jnp
from jax import lax
from jax.experimental import pallas as pl
from jax.experimental.pallas import tpu as pltpu
from jax.sharding import PartitionSpec as P

NAMES = ("yh", "x", "core", "yl", "z")
BLK = 1024
COL = BLK // 2
BF = jnp.bfloat16
F32 = jnp.float32
LIMIT = pltpu.CompilerParams(vmem_limit_bytes=24 * 2**20)


def dot_tn(a, b):
    return lax.dot_general(a, b, (((0,), (0,)), ((), ())), preferred_element_type=F32)


def dot_nt(a, b):
    return lax.dot_general(a, b, (((1,), (1,)), ((), ())), preferred_element_type=F32)


def one_hot_t(ids, groups):
    rows = lax.broadcasted_iota(jnp.int32, (groups, ids.shape[1]), 0)
    return jnp.where(rows == ids, 1.0, 0.0).astype(BF)


def split2(v):
    hi = v.astype(BF)
    return hi, (v - hi.astype(F32)).astype(BF)


def split3(v):
    hi = v.astype(BF)
    rest = v - hi.astype(F32)
    mid = rest.astype(BF)
    return hi, mid, (rest - mid.astype(F32)).astype(BF)


def weighted_kernel(par_ref, ids_ref, c0_ref, c1_ref, x0_ref, x1_ref, out_ref):
    hot = one_hot_t(ids_ref[...], c0_ref.shape[0])
    for i, (c_ref, x_ref) in enumerate(((c0_ref, x0_ref), (c1_ref, x1_ref))):
        rows = dot_tn(hot, c_ref[...])
        out = (rows * x_ref[...].astype(F32)).astype(BF)
        for h in range(2):
            out_ref[h, :, i * COL : (i + 1) * COL] = out[:, h * COL : (h + 1) * COL]


def weighted_call(parity, ids, ctf, particles):
    n, f = particles.shape
    g = ctf.shape[0]
    return pl.pallas_call(
        weighted_kernel,
        grid_spec=pltpu.PrefetchScalarGridSpec(
            num_scalar_prefetch=1,
            grid=(f // BLK // 4,),
            in_specs=[
                pl.BlockSpec((1, n), lambda j, p: (0, 0)),
                pl.BlockSpec((g, BLK), lambda j, p: (0, 4 * j + p[0])),
                pl.BlockSpec((g, BLK), lambda j, p: (0, 4 * j + 2 + p[0])),
                pl.BlockSpec((n, BLK), lambda j, p: (0, 4 * j + p[0])),
                pl.BlockSpec((n, BLK), lambda j, p: (0, 4 * j + 2 + p[0])),
            ],
            out_specs=pl.BlockSpec((2, n, BLK), lambda j, p: (0, 0, j)),
        ),
        out_shape=jax.ShapeDtypeStruct((2, n, f // 4), BF),
        compiler_params=LIMIT,
    )(parity, ids, ctf, ctf, particles, particles)


def score_kernel(with_norms, half_ref, wa_ref, wb_ref, p0_ref, p1_ref, *refs):
    s_ref = refs[-2] if with_norms else refs[-1]
    j = pl.program_id(0)
    n = wa_ref.shape[1]
    proj = jnp.where(j == 0, p0_ref[...], p1_ref[...])
    updates = [
        (s_ref, slice(0, n), dot_nt(wa_ref[0], proj)),
        (s_ref, slice(n, 2 * n), dot_nt(wb_ref[0], proj)),
    ]
    if with_norms:
        poses = proj.shape[0]
        g = refs[0].shape[1]
        c = refs[0][0].astype(F32)
        pf = proj.astype(F32)
        quad = dot_nt(
            jnp.concatenate(split2(c * c), axis=0), jnp.concatenate(split2(pf * pf), axis=0)
        )
        dn = (quad[:g, :poses] + quad[g:, :poses]) + (quad[:g, poses:] + quad[g:, poses:])
        updates.append((refs[-1], slice(0, g), dn))

    @pl.when(j == 0)
    def _():
        for ref, rows, v in updates:
            ref[rows, :] = v

    @pl.when(j > 0)
    def _():
        for ref, rows, v in updates:
            ref[rows, :] += v


def score_call(half, own, recv, pieces, ctf=None):
    _, n, f = own.shape
    poses = pieces[0].shape[0]
    wide = f // 2
    ops = [own, recv, *pieces]

    def part(v):
        return pl.BlockSpec((1, v.shape[1], wide), lambda j, h: (h[0], 0, j))

    specs = [part(own), part(recv)]
    if len(pieces) == 1:
        ops = [own, recv, pieces[0], pieces[0]]
        specs += [pl.BlockSpec((poses, wide), lambda j, h, i=i: (0, i)) for i in range(2)]
    else:
        specs += [pl.BlockSpec((poses, wide), lambda j, h: (0, 0))] * 2
    outs = [jax.ShapeDtypeStruct((2 * n, poses), F32)]
    if ctf is not None:
        ops.append(ctf)
        specs.append(part(ctf))
        outs.append(jax.ShapeDtypeStruct((ctf.shape[1], poses), F32))
    return pl.pallas_call(
        functools.partial(score_kernel, ctf is not None),
        grid_spec=pltpu.PrefetchScalarGridSpec(
            num_scalar_prefetch=1,
            grid=(2,),
            in_specs=specs,
            out_specs=[pl.BlockSpec(o.shape, lambda j, h: (0, 0)) for o in outs],
        ),
        out_shape=outs,
        compiler_params=LIMIT,
    )(half, *ops)


def softmax_kernel(inverse, ids_ref, s0, s1, r_ref, norm_ref, log_ref, w_ref, mass_ref):
    n = s0.shape[0] // 2
    g = norm_ref.shape[0]
    mine, got = s0[...] + s1[...], r_ref[...]
    raw = mine + jnp.concatenate([got[n:], got[:n]], axis=0)
    hot = one_hot_t(ids_ref[...], g)
    picked = dot_tn(
        jnp.concatenate([hot, hot, hot], axis=0), jnp.concatenate(split3(norm_ref[...]), axis=0)
    )
    scores = inverse * (raw - 0.5 * picked)
    peak = jnp.max(scores, axis=1, keepdims=True)
    log_norm = peak + jnp.log(jnp.sum(jnp.exp(scores - peak), axis=1, keepdims=True))
    weights = jnp.exp(scores - log_norm).astype(BF)
    log_ref[...] = log_norm[: log_ref.shape[0], :]
    w_ref[...] = weights
    mh, mm, ml = split3(jnp.dot(hot, weights, preferred_element_type=F32))
    mass_ref[...] = jnp.concatenate([mh, mh, mm, mm, ml], axis=0)


def softmax_call(inverse, ids, s0, s1, got, norms):
    rows = ids.shape[1]
    g, poses = norms.shape
    return pl.pallas_call(
        functools.partial(softmax_kernel, inverse),
        out_shape=[
            jax.ShapeDtypeStruct((rows // 2, 1), F32),
            jax.ShapeDtypeStruct((rows, poses), BF),
            jax.ShapeDtypeStruct((5 * g, poses), BF),
        ],
        compiler_params=LIMIT,
    )(ids, s0, s1, got, norms)


def gradient_kernel(w_ref, mass_ref, wa_ref, wb_ref, p_ref, ctf_ref, out_ref):
    n = wa_ref.shape[1]
    rows = out_ref.shape[3]
    for x in range(4):
        cols = slice(x * COL, (x + 1) * COL)
        acc = dot_tn(w_ref[:n, :], wa_ref[0, :, cols]) + dot_tn(w_ref[n:, :], wb_ref[0, :, cols])
        c = ctf_ref[0, :, cols].astype(F32)
        ch, cl = split2(c * c)
        corr = dot_tn(mass_ref[...], jnp.concatenate([ch, cl, ch, cl, ch], axis=0))
        v = (acc - p_ref[:, cols].astype(F32) * corr).astype(BF)
        for yl in range(2):
            out_ref[0, yl, x] = v[yl * rows : (yl + 1) * rows]


def gradient_call(h, weights, mass, wa, wb, proj, ctf):
    _, n, f = wa.shape
    poses = proj.shape[0]
    wide = f // 2

    def part(v):
        return pl.BlockSpec((1, v.shape[1], wide), lambda a: (h, 0, a))

    def whole(v):
        return pl.BlockSpec(v.shape, lambda a: (0, 0))

    return pl.pallas_call(
        gradient_kernel,
        grid=(2,),
        in_specs=[
            whole(weights),
            whole(mass),
            part(wa),
            part(wb),
            pl.BlockSpec((poses, wide), lambda a: (0, a)),
            part(ctf),
        ],
        out_specs=pl.BlockSpec((1, 2, 4, poses // 2, COL), lambda a: (a, 0, 0, 0, 0)),
        out_shape=jax.ShapeDtypeStruct((2, 2, 4, poses // 2, COL), BF),
        compiler_params=LIMIT,
    )(weights, mass, wa, wb, proj, ctf)


def flip_x(v, bits):
    return lax.ppermute(v, "x", [(i ^ bits, i) for i in range(4)])


def flip_core(v):
    return lax.ppermute(v, "core", [(0, 1), (1, 0)])


def f32(v):
    return v.astype(F32)


def shards(particles, projections, ctf, group_ids):
    n, f = particles.shape
    rows = projections.shape[0]
    nz = lax.axis_size("z")
    poses = rows * nz * 2
    inverse = 4.0 / math.sqrt(f)
    factor = poses / (n * 16 * 2 * nz)
    core = lax.axis_index("core")
    odd = lax.axis_index("x") % 2
    parity = core[None].astype(jnp.int32)
    half = odd[None].astype(jnp.int32)
    ids = group_ids[None, :]

    nb = f // BLK // 2
    quarter = lax.dynamic_slice(
        projections.reshape(rows, nb, 4, COL), (0, 0, 2 * core + odd, 0), (rows, nb, 1, COL)
    ).reshape(rows, nb * COL)
    copies = jnp.broadcast_to(quarter, (2 * nz, rows, nb * COL))
    own = lax.all_to_all(copies, ("yl", "z"), 0, 0).reshape(poses, nb * COL)
    w_own = weighted_call(parity, ids, ctf, particles)
    ids_oth = flip_core(ids)
    w_recv = weighted_call(parity, ids_oth, ctf, flip_core(particles))
    ids_all = jnp.concatenate([ids, ids_oth], axis=1)
    ctf_own = lax.dynamic_index_in_dim(
        ctf.reshape(ctf.shape[0], nb, 2, 2, COL), core, axis=2, keepdims=False
    )
    ctf_own = ctf_own.transpose(2, 0, 1, 3).reshape(2, ctf.shape[0], nb * COL)

    own, w_own, w_recv, ids_all, ctf_own = lax.optimization_barrier(
        (own, w_own, w_recv, ids_all, ctf_own)
    )

    mid = nb * COL // 2
    oth = [flip_x(own[:, :mid], 1), flip_x(own[:, mid:], 3)]

    w_own = pltpu.with_memory_space_constraint(w_own, pltpu.HBM)
    w_recv = pltpu.with_memory_space_constraint(w_recv, pltpu.HBM)
    s0, norms = score_call(half, w_own, w_recv, [own], ctf_own)
    norms = norms + flip_core(norms)
    norms = norms + flip_x(norms, 1)
    (s1,) = score_call(1 - half, w_own, w_recv, oth)
    got = flip_core(s0 + s1)
    log_norm, weights, mass = softmax_call(inverse, ids_all, s0, s1, got, norms)

    last = []
    for h in range(2):
        proj = jnp.where(odd == h, own, jnp.concatenate(oth, axis=1))
        part = gradient_call(h, weights, mass, w_own, w_recv, proj, ctf_own)
        part = part.reshape(16, poses // 2, COL)
        part = lax.all_to_all(part, ("yh", "yl", "x"), 0, 0)
        last.append(jnp.sum(f32(part), axis=0).astype(BF))
    last = jnp.concatenate(last, axis=1).reshape(nz, rows, BLK)
    parts = lax.all_to_all(last, "z", 0, 0)
    out = factor * jnp.sum(f32(parts), axis=0)
    return out, log_norm[:, 0]


def solution(mesh):
    fine = jax.sharding.Mesh(mesh.devices.reshape(2, 4, 2, 2, 8), NAMES)
    grp, pose = ("yh", "x", "core"), ("yl", "z")
    return jax.shard_map(
        shards,
        mesh=fine,
        in_specs=(P(grp + pose, None), P(pose, None), P(), P(grp + pose)),
        out_specs=(P(pose, grp), P(grp + pose)),
        check_vma=False,
    )
```

time: 301 us -> 125 us (0.42)
  waiting for transfers between devices: 246 us -> 46.5 us
  matrix products: 40 us -> 0 us
  starting transfers between devices: 0.12 us -> 32.5 us
  Pallas kernels: 0 us -> 24.5 us
  local copies, waits for them, and re-layouts: 0.03 us -> 16.2 us
  between operations: 13.9 us -> 0.84 us
  other arithmetic: 0.24 us -> 3.81 us
    reduce_scatter x2 -> x0, waiting for transfers between devices: 174 us -> none  [the longest x1 98.7 us: shards(): lax.psum_scatter(factor * numerator, 'pose', scatter_dimension=0, tiled=T...]
    all_gather x1 -> x0, waiting for transfers between devices: 72 us -> none  [shards(): gathered = lax.all_gather(projections, 'pose', axis=0, tiled=True)]
    all_to_all x0 -> x4, waiting for transfers between devices: none -> 40.6 us  [the longest x2 26.1 us: shards(): part = lax.all_to_all(part, ('yh', 'yl', 'x'), 0, 0)]
    dot_general x7 -> x0, matrix products: 40 us -> none  [the longest x1 10.2 us: shards(): jnp.dot(pose_mass, ctf_square, precision=high)]
    all_to_all x0 -> x4, starting transfers between devices: none -> 28.1 us  [the longest x2 13.3 us: shards(): part = lax.all_to_all(part, ('yh', 'yl', 'x'), 0, 0)]
    pallas_call x0 -> x7, Pallas kernels: none -> 24.5 us  [the longest x2 8.69 us: gradient_call(): pl.pallas_call(gradient_kernel, grid=(2,), in_specs=[whole(weights), whol...]
    unnamed x14 -> x13, local copies, waits for them, and re-layouts: 0.03 us -> 10.7 us
    ppermute x0 -> x7, waiting for transfers between devices: none -> 5.95 us  [the longest x3 3.39 us: flip_x(): return lax.ppermute(v, 'x', [(i ^ bits, i) for i in range(4)])]
  transfers between devices with their start and end apart: 3 -> 11, of which waited for: 3 -> 8; matrix products, arithmetic and copies ran while one was open for 3% -> 5% of each run, Pallas kernels for 0% -> 13%
where the time goes in v2:
time: 125 us; the launch traced here: 124 us
  waiting for transfers between devices  46.5 us (37%)
  starting transfers between devices  32.5 us (26%)
  Pallas kernels  24.5 us (20%)
  local copies, waits for them, and re-layouts  16.2 us (13%)
  other arithmetic  3.81 us (3%)
    all_to_all x2, waiting for transfers between devices, shards(): part = lax.all_to_all(part, ('yh', 'yl', 'x'), 0, 0)  26.1 us
    all_to_all x2, starting transfers between devices, shards(): part = lax.all_to_all(part, ('yh', 'yl', 'x'), 0, 0)  13.3 us
    unnamed x13, local copies, waits for them, and re-layouts  10.7 us
    all_to_all x1, starting transfers between devices, shards(): own = lax.all_to_all(copies, ('yl', 'z'), 0, 0).reshape(poses, nb * COL)  9.58 us
    pallas_call x2, Pallas kernels, gradient_call(): pl.pallas_call(gradient_kernel, grid=(2,), in_specs=[whole(weights), whol...  8.69 us
    all_to_all x1, waiting for transfers between devices, shards(): parts = lax.all_to_all(last, 'z', 0, 0)  8.35 us
    pallas_call x2, Pallas kernels, weighted_call(): pl.pallas_call(weighted_kernel, grid_spec=pltpu.PrefetchScalarGridSpec(nu...  7.65 us
    pallas_call x2, Pallas kernels, score_call(): pl.pallas_call(functools.partial(score_kernel, ctf is not None), grid_spe...  7.53 us
  transfers between devices with their start and end apart: 11, of which 8 were waited for; matrix products, arithmetic and copies ran while one was open for 5% of the time, Pallas kernels for 13%

profile of v2, /device:TPU:2, one launch (start us, length us, event | category | flops | bytes accessed | tf_op | source)
XLA Modules:
  0.0 124.3 jit_solution(18268145379214689861)
XLA Ops:
  0.6 0.0 copy-start
  0.6 0.1 collective-permute-start.1
  0.8 0.8 copy-done
  1.6 1.1 broadcast_in_dim.12
  2.7 9.6 %all-to-all-start = ((bf16[16,8,4096]{2,1,0:T(8,128)(2,1)}), bf16[16,8,4096]{2,1,0:T(8,128)(2,1)S(1)}, u32[]{:S(2)}, u32[]{:S(2)}) async-start(bf16[16,8,4096]{2,1,0:T(8,128)(2,1)} %broadcast_in_dim.12), calls=%async_computation | async-start | bytes 2097152 | tf_op jit(solution)/shard_map/all_to_all | solution.py:244
  12.3 0.7 broadcast_in_dim.14.ids_ref
  12.9 0.0 collective-permute-start
  12.9 1.8 %reshape.31 = bf16[32,8,2,2,512]{4,3,2,1,0:T(2,128)(2,1)S(1)} reshape(bf16[32,16384]{1,0:T(8,128)(2,1)} %c1_ref.3) | data formatting | bytes 2097152 | tf_op jit(solution)/shard_map/reshape | solution.py:250
  14.8 0.5 constant_dynamic-slice_fusion
  15.2 0.1 copy.10
  15.3 0.2 reshape.32.refs_0_.ctf_ref
  15.6 0.0 copy-start.3
  15.6 4.0 %copy-done.3 = bf16[320,16384]{1,0:T(8,128)(2,1)S(1)} copy-done((bf16[320,16384]{1,0:T(8,128)(2,1)S(1)}, bf16[320,16384]{1,0:T(8,128)(2,1)}, u32[]{:S(2)}) %copy-start.3) | copy-done | bytes 10485784
  19.6 0.0 copy-start.4
  19.6 1.2 copy-done.4
  20.8 0.0 copy-start.5
  20.8 3.0 %shard_map.59.wa_ref = bf16[2,320,4096]{2,1,0:T(8,128)(2,1)S(1)} custom-call(s32[1]{0:T(128)} %bitcast.3.par_ref, s32[1,320]{1,0:T(1,128)S(1)} %broadcast_in_dim.14.ids_ref, bf16[32,16384]{1,0:T(8,128)(2,1)S(1)} %copy-done.4, bf16[32,16384]{1,0:T(8,128)(2,1)S(1)} %copy-done.4, bf16[320,16384]{1,0:T(8,128)(2,1)S(1)} %copy-done.3, bf16[320,16384]{1,0:T(8,128)(2,1)S(1)} %copy-done.3), custom_call_target="tpu_custom_call" | custom-call | tf_op jit(solution)/shard_map/pallas_call | solution.py:56
  23.8 0.0 copy-start.1
  23.8 2.3 %copy-done.1 = bf16[2,320,4096]{2,1,0:T(8,128)(2,1)} copy-done((bf16[2,320,4096]{2,1,0:T(8,128)(2,1)}, bf16[2,320,4096]{2,1,0:T(8,128)(2,1)S(1)}, u32[]{:S(2)}) %copy-start.1) | copy-done | bytes 5242904
  26.1 0.0 collective-permute-done.ids_ref
  26.1 0.1 pad_add_fusion.ids_ref
  26.2 0.0 collective-permute-done.1.x0_ref.x1_ref
  26.2 0.0 copy-done.5
  26.2 4.7 %shard_map.60.wb_ref = bf16[2,320,4096]{2,1,0:T(8,128)(2,1)S(1)} custom-call(s32[1]{0:T(128)} %bitcast.3.par_ref, s32[1,320]{1,0:T(1,128)S(1)} %collective-permute-done.ids_ref, bf16[32,16384]{1,0:T(8,128)(2,1)S(1)} %copy-done.5, bf16[32,16384]{1,0:T(8,128)(2,1)S(1)} %copy-done.5, bf16[320,16384]{1,0:T(8,128)(2,1)} %collective-permute-done.1.x0_ref.x1_ref, ...), custom_call_target="tpu_custom_call" | custom-call | tf_op jit(solution)/shard_map/pallas_call | solution.py:56
  30.9 0.0 copy-start.2
  30.9 2.3 %copy-done.2 = bf16[2,320,4096]{2,1,0:T(8,128)(2,1)} copy-done((bf16[2,320,4096]{2,1,0:T(8,128)(2,1)}, bf16[2,320,4096]{2,1,0:T(8,128)(2,1)S(1)}, u32[]{:S(2)}) %copy-start.2) | copy-done | bytes 5242904
  33.2 6.1 %all-to-all-done = bf16[16,8,4096]{2,1,0:T(8,128)(2,1)S(1)} async-done(((bf16[16,8,4096]{2,1,0:T(8,128)(2,1)}), bf16[16,8,4096]{2,1,0:T(8,128)(2,1)S(1)}, u32[]{:S(2)}, u32[]{:S(2)}) %all-to-all-start) | async-done | bytes 1048608 | tf_op jit(solution)/shard_map/all_to_all | solution.py:244
  39.3 1.1 fusion
  40.4 0.5 collective-permute-start.2
  40.9 2.2 %collective-permute-start.3 = (bf16[128,2048]{1,0:T(8,128)(2,1)}, bf16[128,2048]{1,0:T(8,128)(2,1)S(1)}, u32[]{:S(2)}, u32[]{:S(2)}) collective-permute-start(bf16[128,2048]{1,0:T(8,128)(2,1)} %get-tuple-element.24), channel_id=1, source_target_pairs={{96,0},{64,32},{32,64},{0,96},{97,1},{65,33},{33,65},{1,97},{98,2}... | collective-permute-start | bytes 1572872 | tf_op jit(solution)/shard_map/ppermute | solution.py:215
  43.1 4.1 %shard_map.61 = (f32[640,128]{1,0:T(8,128)S(1)}, f32[32,128]{1,0:T(8,128)S(1)}) custom-call(s32[1]{0:T(128)} %bitcast.6.half_ref, bf16[2,320,4096]{2,1,0:T(8,128)(2,1)} %copy-done.1, bf16[2,320,4096]{2,1,0:T(8,128)(2,1)} %copy-done.2, bf16[128,4096]{1,0:T(8,128)(2,1)S(1)} %bitcast.18, bf16[128,4096]{1,0:T(8,128)(2,1)S(1)} %bitcast.19, ...), custom_call_target="tpu_custom_call" | custom-call | tf_op jit(solution)/shard_map/pallas_call | solution.py:126
  47.2 0.1 collective-permute-start.5
  47.3 1.2 collective-permute-done.5
  48.4 1.4 %collective-permute-start.6 = (f32[32,128]{1,0:T(8,128)S(1)}, f32[32,128]{1,0:T(8,128)S(1)}, u32[]{:S(2)}, u32[]{:S(2)}) collective-permute-start(f32[32,128]{1,0:T(8,128)S(1)} %add.28), channel_id=1, source_target_pairs={{32,0},{0,32},{96,64},{64,96},{33,1},{1,33},{97,65},{65,97},{34,2}... | collective-permute-start | bytes 49160 | tf_op jit(solution)/shard_map/ppermute | solution.py:215
  49.9 3.1 %collective-permute-done.6 = f32[32,128]{1,0:T(8,128)S(1)} collective-permute-done((f32[32,128]{1,0:T(8,128)S(1)}, f32[32,128]{1,0:T(8,128)S(1)}, u32[]{:S(2)}, u32[]{:S(2)}) %collective-permute-start.6) | collective-permute-done | bytes 16416 | tf_op jit(solution)/shard_map/ppermute | solution.py:215
  53.0 0.0 collective-permute-done.2.p0_ref
  53.0 0.3 collective-permute-done.3.p1_ref
  53.3 3.5 %shard_map.62.s1 = f32[640,128]{1,0:T(8,128)S(1)} custom-call(s32[1]{0:T(128)S(6)} %sub.3.half_ref, bf16[2,320,4096]{2,1,0:T(8,128)(2,1)} %copy-done.1, bf16[2,320,4096]{2,1,0:T(8,128)(2,1)} %copy-done.2, bf16[128,2048]{1,0:T(8,128)(2,1)S(1)} %collective-permute-done.2.p0_ref, bf16[128,2048]{1,0:T(8,128)(2,1)S(1)} %collective-permute-done.3.p1_ref), custom_call_target="tpu_custom_call" | custom-call | tf_op jit(solution)/shard_map/pallas_call | solution.py:126
  56.8 0.1 collective-permute-start.4
  57.0 0.1 broadcast_select_fusion.1
  57.1 1.4 %collective-permute-done.4.r_ref = f32[640,128]{1,0:T(8,128)S(1)} collective-permute-done((f32[640,128]{1,0:T(8,128)S(1)}, f32[640,128]{1,0:T(8,128)S(1)}, u32[]{:S(2)}, u32[]{:S(2)}) %collective-permute-start.4) | collective-permute-done | bytes 327712 | tf_op jit(solution)/shard_map/ppermute | solution.py:219
  58.5 0.6 shard_map.63
  59.1 4.4 %shard_map.64 = bf16[2,2,4,64,512]{4,3,2,1,0:T(8,128)(2,1)} custom-call(bf16[640,128]{1,0:T(8,128)(2,1)S(1)} %get-tuple-element.19.w_ref, bf16[160,128]{1,0:T(8,128)(2,1)S(1)} %get-tuple-element.20.mass_ref, bf16[2,320,4096]{2,1,0:T(8,128)(2,1)} %copy-done.1, bf16[2,320,4096]{2,1,0:T(8,128)(2,1)} %copy-done.2, ...), custom_call_target="tpu_custom_call" | custom-call | tf_op jit(solution)/shard_map/pallas_call | solution.py:197
  63.5 8.0 %all-to-all-start.1 = ((bf16[16,64,512]{2,1,0:T(8,128)(2,1)}), bf16[16,64,512]{2,1,0:T(8,128)(2,1)}, u32[]{:S(2)}, u32[]{:S(2)}) async-start(bf16[16,64,512]{2,1,0:T(8,128)(2,1)} %bitcast.7), calls=%async_computation.1 | async-start | bytes 2097152 | tf_op jit(solution)/shard_map/all_to_all | solution.py:275
  71.5 4.3 %shard_map.65 = bf16[2,2,4,64,512]{4,3,2,1,0:T(8,128)(2,1)} custom-call(bf16[640,128]{1,0:T(8,128)(2,1)S(1)} %get-tuple-element.19.w_ref, bf16[160,128]{1,0:T(8,128)(2,1)S(1)} %get-tuple-element.20.mass_ref, bf16[2,320,4096]{2,1,0:T(8,128)(2,1)} %copy-done.1, bf16[2,320,4096]{2,1,0:T(8,128)(2,1)} %copy-done.2, ...), custom_call_target="tpu_custom_call" | custom-call | tf_op jit(solution)/shard_map/pallas_call | solution.py:197
  75.8 11.9 %all-to-all-done.1 = bf16[16,64,512]{2,1,0:T(8,128)(2,1)} async-done(((bf16[16,64,512]{2,1,0:T(8,128)(2,1)}), bf16[16,64,512]{2,1,0:T(8,128)(2,1)}, u32[]{:S(2)}, u32[]{:S(2)}) %all-to-all-start.1) | async-done | bytes 1048608 | tf_op jit(solution)/shard_map/all_to_all | solution.py:275
  87.7 5.2 %all-to-all-start.2 = ((bf16[16,64,512]{2,1,0:T(8,128)(2,1)}), bf16[16,64,512]{2,1,0:T(8,128)(2,1)S(1)}, u32[]{:S(2)}, u32[]{:S(2)}) async-start(bf16[16,64,512]{2,1,0:T(8,128)(2,1)} %bitcast.8), calls=%async_computation.2 | async-start | bytes 2097152 | tf_op jit(solution)/shard_map/all_to_all | solution.py:275
  93.0 1.4 %reduce_sum.33 = bf16[64,512]{1,0:T(8,128)(2,1)S(1)} reduce(bf16[16,64,512]{2,1,0:T(8,128)(2,1)} %all-to-all-done.1, bf16[]{:T(256)} %constant.39.clone.1), dimensions={0}, to_apply=%region_0.1 | reduce | flops 491520 | bytes 1114114 | tf_op jit(solution)/shard_map/reduce_sum | solution.py:276
  94.3 14.2 %all-to-all-done.2 = bf16[16,64,512]{2,1,0:T(8,128)(2,1)S(1)} async-done(((bf16[16,64,512]{2,1,0:T(8,128)(2,1)}), bf16[16,64,512]{2,1,0:T(8,128)(2,1)S(1)}, u32[]{:S(2)}, u32[]{:S(2)}) %all-to-all-start.2) | async-done | bytes 1048608 | tf_op jit(solution)/shard_map/all_to_all | solution.py:275
  108.6 0.1 reduce_sum.34
  108.7 0.7 maximum_bitcast_fusion
  109.4 5.2 %all-to-all-start.3 = ((bf16[8,8,1024]{2,1,0:T(8,128)(2,1)}), bf16[8,8,1024]{2,1,0:T(8,128)(2,1)S(1)}, u32[]{:S(2)}, u32[]{:S(2)}) async-start(bf16[8,8,1024]{2,1,0:T(8,128)(2,1)} %maximum_bitcast_fusion), calls=%async_computation.3 | async-start | bytes 262144 | tf_op jit(solution)/shard_map/all_to_all | solution.py:278
  114.6 0.7 reduce.2
  115.3 8.4 %all-to-all-done.3 = bf16[8,8,1024]{2,1,0:T(8,128)(2,1)S(1)} async-done(((bf16[8,8,1024]{2,1,0:T(8,128)(2,1)}), bf16[8,8,1024]{2,1,0:T(8,128)(2,1)S(1)}, u32[]{:S(2)}, u32[]{:S(2)}) %all-to-all-start.3) | async-done | bytes 131104 | tf_op jit(solution)/shard_map/all_to_all | solution.py:278
  123.7 0.6 broadcast_multiply_fusion
  (7 shorter events, 0.1 us)
Async XLA Ops:
  0.6 1.0 copy-start
  0.6 25.6 %collective-permute-start.1 = (bf16[320,16384]{1,0:T(8,128)(2,1)}, bf16[320,16384]{1,0:T(8,128)(2,1)}, u32[]{:S(2)}, u32[]{:S(2)}) collective-permute-start(bf16[320,16384]{1,0:T(8,128)(2,1)} %x1_ref.1), channel_id=1, source_target_pairs={{0,16},{16,0},{1,17},{17,1},{2,18},{18,2},{3,19},{19,3},{4,20},{20... | collective-permute-start | bytes 31457288 | tf_op jit(solution)/shard_map/ppermute | solution.py:219
  2.7 36.7 %all-to-all-start = ((bf16[16,8,4096]{2,1,0:T(8,128)(2,1)}), bf16[16,8,4096]{2,1,0:T(8,128)(2,1)S(1)}, u32[]{:S(2)}, u32[]{:S(2)}) async-start(bf16[16,8,4096]{2,1,0:T(8,128)(2,1)} %broadcast_in_dim.12), calls=%async_computation | async-start | bytes 2097152 | tf_op jit(solution)/shard_map/all_to_all | solution.py:244
  12.9 13.2 %collective-permute-start = (s32[1,320]{1,0:T(1,128)S(1)}, s32[1,320]{1,0:T(1,128)S(1)}, u32[]{:S(2)}, u32[]{:S(2)}) collective-permute-start(s32[1,320]{1,0:T(1,128)S(1)} %broadcast_in_dim.14.ids_ref), channel_id=1, source_target_pairs={{0,16},{16,0},{1,17},{17,1},{2,18},{18,2},{3,19},{19,3},{4,20},{20... | collective-permute-start | bytes 3848 | tf_op jit(solution)/shard_map/ppermute | solution.py:219
  15.6 4.0 %copy-start.3 = (bf16[320,16384]{1,0:T(8,128)(2,1)S(1)}, bf16[320,16384]{1,0:T(8,128)(2,1)}, u32[]{:S(2)}) copy-start(bf16[320,16384]{1,0:T(8,128)(2,1)} %x1_ref.1) | copy-start | bytes 31457284
  19.6 1.2 copy-start.4
  20.8 5.4 %copy-start.5 = (bf16[32,16384]{1,0:T(8,128)(2,1)S(1)}, bf16[32,16384]{1,0:T(8,128)(2,1)}, u32[]{:S(2)}) copy-start(bf16[32,16384]{1,0:T(8,128)(2,1)} %c1_ref.3) | copy-start | bytes 3145732
  23.8 2.4 %copy-start.1 = (bf16[2,320,4096]{2,1,0:T(8,128)(2,1)}, bf16[2,320,4096]{2,1,0:T(8,128)(2,1)S(1)}, u32[]{:S(2)}) copy-start(bf16[2,320,4096]{2,1,0:T(8,128)(2,1)S(1)} %shard_map.59.wa_ref) | copy-start | bytes 15728644
  30.9 2.3 %copy-start.2 = (bf16[2,320,4096]{2,1,0:T(8,128)(2,1)}, bf16[2,320,4096]{2,1,0:T(8,128)(2,1)S(1)}, u32[]{:S(2)}) copy-start(bf16[2,320,4096]{2,1,0:T(8,128)(2,1)S(1)} %shard_map.60.wb_ref) | copy-start | bytes 15728644
  40.4 12.6 %collective-permute-start.2 = (bf16[128,2048]{1,0:T(8,128)(2,1)}, bf16[128,2048]{1,0:T(8,128)(2,1)S(1)}, u32[]{:S(2)}, u32[]{:S(2)}) collective-permute-start(bf16[128,2048]{1,0:T(8,128)(2,1)} %get-tuple-element.25), channel_id=1, source_target_pairs={{32,0},{0,32},{96,64},{64,96},{33,1},{1,33},{97,65},{65,97},{34,2}... | collective-permute-start | bytes 1572872 | tf_op jit(solution)/shard_map/ppermute | solution.py:215
  40.9 12.3 %collective-permute-start.3 = (bf16[128,2048]{1,0:T(8,128)(2,1)}, bf16[128,2048]{1,0:T(8,128)(2,1)S(1)}, u32[]{:S(2)}, u32[]{:S(2)}) collective-permute-start(bf16[128,2048]{1,0:T(8,128)(2,1)} %get-tuple-element.24), channel_id=1, source_target_pairs={{96,0},{64,32},{32,64},{0,96},{97,1},{65,33},{33,65},{1,97},{98,2}... | collective-permute-start | bytes 1572872 | tf_op jit(solution)/shard_map/ppermute | solution.py:215
  47.2 1.3 %collective-permute-start.5 = (f32[32,128]{1,0:T(8,128)S(1)}, f32[32,128]{1,0:T(8,128)S(1)}, u32[]{:S(2)}, u32[]{:S(2)}) collective-permute-start(f32[32,128]{1,0:T(8,128)S(1)} %get-tuple-element.18), channel_id=1, source_target_pairs={{0,16},{16,0},{1,17},{17,1},{2,18},{18,2},{3,19},{19,3},{4,20},{20... | collective-permute-start | bytes 49160 | tf_op jit(solution)/shard_map/ppermute | solution.py:219
  48.4 4.5 %collective-permute-start.6 = (f32[32,128]{1,0:T(8,128)S(1)}, f32[32,128]{1,0:T(8,128)S(1)}, u32[]{:S(2)}, u32[]{:S(2)}) collective-permute-start(f32[32,128]{1,0:T(8,128)S(1)} %add.28), channel_id=1, source_target_pairs={{32,0},{0,32},{96,64},{64,96},{33,1},{1,33},{97,65},{65,97},{34,2}... | collective-permute-start | bytes 49160 | tf_op jit(solution)/shard_map/ppermute | solution.py:215
  56.8 1.7 %collective-permute-start.4 = (f32[640,128]{1,0:T(8,128)S(1)}, f32[640,128]{1,0:T(8,128)S(1)}, u32[]{:S(2)}, u32[]{:S(2)}) collective-permute-start(f32[640,128]{1,0:T(8,128)S(1)} %add.27), channel_id=1, source_target_pairs={{0,16},{16,0},{1,17},{17,1},{2,18},{18,2},{3,19},{19,3},{4,20},{20... | collective-permute-start | bytes 983048 | tf_op jit(solution)/shard_map/ppermute | solution.py:219
  63.5 24.2 %all-to-all-start.1 = ((bf16[16,64,512]{2,1,0:T(8,128)(2,1)}), bf16[16,64,512]{2,1,0:T(8,128)(2,1)}, u32[]{:S(2)}, u32[]{:S(2)}) async-start(bf16[16,64,512]{2,1,0:T(8,128)(2,1)} %bitcast.7), calls=%async_computation.1 | async-start | bytes 2097152 | tf_op jit(solution)/shard_map/all_to_all | solution.py:275
  87.7 20.8 %all-to-all-start.2 = ((bf16[16,64,512]{2,1,0:T(8,128)(2,1)}), bf16[16,64,512]{2,1,0:T(8,128)(2,1)S(1)}, u32[]{:S(2)}, u32[]{:S(2)}) async-start(bf16[16,64,512]{2,1,0:T(8,128)(2,1)} %bitcast.8), calls=%async_computation.2 | async-start | bytes 2097152 | tf_op jit(solution)/shard_map/all_to_all | solution.py:275
  109.4 14.3 %all-to-all-start.3 = ((bf16[8,8,1024]{2,1,0:T(8,128)(2,1)}), bf16[8,8,1024]{2,1,0:T(8,128)(2,1)S(1)}, u32[]{:S(2)}, u32[]{:S(2)}) async-start(bf16[8,8,1024]{2,1,0:T(8,128)(2,1)} %maximum_bitcast_fusion), calls=%async_computation.3 | async-start | bytes 262144 | tf_op jit(solution)/shard_map/all_to_all | solution.py:278

commit v3 on v2

v3 whole, which is shorter than its diff:
```python
import functools
import math

import jax
import jax.numpy as jnp
from jax import lax
from jax.experimental import pallas as pl
from jax.experimental.pallas import tpu as pltpu
from jax.sharding import PartitionSpec as P

NAMES = ("yh", "x", "core", "yl", "z")
BLK = 1024
COL = BLK // 2
BF = jnp.bfloat16
F32 = jnp.float32
LIMIT = pltpu.CompilerParams(vmem_limit_bytes=24 * 2**20)


def dot_tn(a, b):
    return lax.dot_general(a, b, (((0,), (0,)), ((), ())), preferred_element_type=F32)


def dot_nt(a, b):
    return lax.dot_general(a, b, (((1,), (1,)), ((), ())), preferred_element_type=F32)


def one_hot_t(ids, groups):
    rows = lax.broadcasted_iota(jnp.int32, (groups, ids.shape[1]), 0)
    return jnp.where(rows == ids, 1.0, 0.0).astype(BF)


def split2(v):
    hi = v.astype(BF)
    return hi, (v - hi.astype(F32)).astype(BF)


def split3(v):
    hi = v.astype(BF)
    rest = v - hi.astype(F32)
    mid = rest.astype(BF)
    return hi, mid, (rest - mid.astype(F32)).astype(BF)


def weighted_kernel(par_ref, ids_ref, c0_ref, c1_ref, x0_ref, x1_ref, out_ref):
    hot = one_hot_t(ids_ref[...], c0_ref.shape[0])
    for i, (c_ref, x_ref) in enumerate(((c0_ref, x0_ref), (c1_ref, x1_ref))):
        rows = dot_tn(hot, c_ref[...])
        out = (rows * x_ref[...].astype(F32)).astype(BF)
        for h in range(2):
            out_ref[h, :, i * COL : (i + 1) * COL] = out[:, h * COL : (h + 1) * COL]


def weighted_call(parity, ids, ctf, particles):
    n, f = particles.shape
    g = ctf.shape[0]
    return pl.pallas_call(
        weighted_kernel,
        grid_spec=pltpu.PrefetchScalarGridSpec(
            num_scalar_prefetch=1,
            grid=(f // BLK // 4,),
            in_specs=[
                pl.BlockSpec((1, n), lambda j, p: (0, 0)),
                pl.BlockSpec((g, BLK), lambda j, p: (0, 4 * j + p[0])),
                pl.BlockSpec((g, BLK), lambda j, p: (0, 4 * j + 2 + p[0])),
                pl.BlockSpec((n, BLK), lambda j, p: (0, 4 * j + p[0])),
                pl.BlockSpec((n, BLK), lambda j, p: (0, 4 * j + 2 + p[0])),
            ],
            out_specs=pl.BlockSpec((2, n, BLK), lambda j, p: (0, 0, j)),
        ),
        out_shape=pltpu.HBM((2, n, f // 4), BF),
        compiler_params=LIMIT,
    )(parity, ids, ctf, ctf, particles, particles)


def score_kernel(at_ref, wa_ref, wb_ref, p0_ref, p1_ref, c0, c1, c2, c3, s_ref):
    j = pl.program_id(0)
    n = wa_ref.shape[1]
    g, poses = c0.shape[0], p0_ref.shape[0]
    proj = jnp.where(j == 0, p0_ref[...], p1_ref[...])
    c = jnp.concatenate([r[...] for r in (c0, c1, c2, c3)], axis=1).astype(F32)
    pf = proj.astype(F32)
    quad = dot_nt(jnp.concatenate(split2(c * c), axis=0), jnp.concatenate(split2(pf * pf), axis=0))
    updates = (
        (slice(0, n), dot_nt(wa_ref[0], proj)),
        (slice(n, 2 * n), dot_nt(wb_ref[0], proj)),
        (
            slice(2 * n, 2 * n + g),
            (quad[:g, :poses] + quad[g:, :poses]) + (quad[:g, poses:] + quad[g:, poses:]),
        ),
    )

    @pl.when(j == 0)
    def _():
        for rows, v in updates:
            s_ref[rows, :] = v

    @pl.when(j > 0)
    def _():
        for rows, v in updates:
            s_ref[rows, :] += v


def score_call(half, parity, own, recv, pieces, ctf):
    _, n, f = own.shape
    poses = pieces[0].shape[0]
    g = ctf.shape[0]
    wide = f // 2
    part = pl.BlockSpec((1, n, wide), lambda j, t: (t[0], 0, j))
    if len(pieces) == 1:
        pieces = pieces * 2
        specs = [pl.BlockSpec((poses, wide), lambda j, t, i=i: (0, i)) for i in range(2)]
    else:
        specs = [pl.BlockSpec((poses, wide), lambda j, t: (0, 0))] * 2
    specs += [
        pl.BlockSpec((g, COL), lambda j, t, i=i: (0, 4 * (4 * j + i) + 2 * t[1] + t[0])) for i in range(4)
    ]
    return pl.pallas_call(
        score_kernel,
        grid_spec=pltpu.PrefetchScalarGridSpec(
            num_scalar_prefetch=1,
            grid=(2,),
            in_specs=[part, part, *specs],
            out_specs=pl.BlockSpec((2 * n + g, poses), lambda j, t: (0, 0)),
        ),
        out_shape=jax.ShapeDtypeStruct((2 * n + g, poses), F32),
        compiler_params=LIMIT,
    )(jnp.concatenate([half, parity]), own, recv, *pieces, ctf, ctf, ctf, ctf)


def softmax_kernel(inverse, ids_ref, s_ref, r_ref, log_ref, w_ref, mass_ref):
    n = log_ref.shape[0]
    g = s_ref.shape[0] - 2 * n
    mine, got = s_ref[...], r_ref[...]
    raw = mine[: 2 * n] + jnp.concatenate([got[n : 2 * n], got[:n]], axis=0)
    norms = mine[2 * n :] + got[2 * n :]
    hot = one_hot_t(ids_ref[...], g)
    picked = dot_tn(
        jnp.concatenate([hot, hot, hot], axis=0), jnp.concatenate(split3(norms), axis=0)
    )
    scores = inverse * (raw - 0.5 * picked)
    peak = jnp.max(scores, axis=1, keepdims=True)
    log_norm = peak + jnp.log(jnp.sum(jnp.exp(scores - peak), axis=1, keepdims=True))
    weights = jnp.exp(scores - log_norm).astype(BF)
    log_ref[...] = log_norm[: log_ref.shape[0], :]
    w_ref[...] = weights
    mh, mm, ml = split3(jnp.dot(hot, weights, preferred_element_type=F32))
    mass_ref[...] = jnp.concatenate([mh, mh, mm, mm, ml], axis=0)


def softmax_call(inverse, ids, mine, got):
    rows = ids.shape[1]
    g, poses = mine.shape[0] - rows, mine.shape[1]
    return pl.pallas_call(
        functools.partial(softmax_kernel, inverse),
        out_shape=[
            jax.ShapeDtypeStruct((rows // 2, 1), F32),
            jax.ShapeDtypeStruct((rows, poses), BF),
            jax.ShapeDtypeStruct((5 * g, poses), BF),
        ],
        compiler_params=LIMIT,
    )(ids, mine, got)


def gradient_kernel(at_ref, w_ref, mass_ref, wa_ref, wb_ref, p0_ref, p1_ref, c0, c1, c2, c3, out_ref):
    n = wa_ref.shape[1]
    rows = out_ref.shape[3]
    own = pl.program_id(0) == at_ref[0]
    for x, c_ref in enumerate((c0, c1, c2, c3)):
        cols = slice(x * COL, (x + 1) * COL)
        acc = dot_tn(w_ref[:n, :], wa_ref[0, :, cols]) + dot_tn(w_ref[n:, :], wb_ref[0, :, cols])
        c = c_ref[...].astype(F32)
        ch, cl = split2(c * c)
        corr = dot_tn(mass_ref[...], jnp.concatenate([ch, cl, ch, cl, ch], axis=0))
        proj = jnp.where(own, p0_ref[:, cols], p1_ref[:, cols])
        v = (acc - proj.astype(F32) * corr).astype(BF)
        for i in range(2):
            out_ref[0, at_ref[2] ^ i, x] = v[i * rows : (i + 1) * rows]


def gradient_call(at, weights, mass, wa, wb, own, oth, ctf):
    _, n, f = wa.shape
    poses = own.shape[0]
    wide = f // 2
    g = ctf.shape[0]

    def whole(v):
        return pl.BlockSpec(v.shape, lambda h, a, t: (0, 0))

    part = pl.BlockSpec((1, n, wide), lambda h, a, t: (h, 0, a))
    proj = pl.BlockSpec((poses, wide), lambda h, a, t: (0, a))
    ctfs = [
        pl.BlockSpec((g, COL), lambda h, a, t, i=i: (0, 4 * (4 * a + i) + 2 * t[1] + h)) for i in range(4)
    ]
    return pl.pallas_call(
        gradient_kernel,
        grid_spec=pltpu.PrefetchScalarGridSpec(
            num_scalar_prefetch=1,
            grid=(2, 2),
            in_specs=[whole(weights), whole(mass), part, part, proj, proj, *ctfs],
            out_specs=pl.BlockSpec((1, 2, 4, poses // 2, COL), lambda h, a, t: (a, 0, 0, 0, h)),
        ),
        out_shape=pltpu.VMEM((2, 2, 4, poses // 2, BLK), BF),
        compiler_params=LIMIT,
    )(at, weights, mass, wa, wb, own, oth, ctf, ctf, ctf, ctf)


def copies_kernel(nb, at_ref, p_ref, out_ref):
    for j in range(nb):
        cols = pl.ds(pl.multiple_of((4 * j + at_ref[0]) * COL, COL), COL)
        v = p_ref[:, cols]
        for i in range(out_ref.shape[0]):
            out_ref[i, :, j * COL : (j + 1) * COL] = v


def copies_call(at, projections, nb, count):
    rows = projections.shape[0]
    return pl.pallas_call(
        functools.partial(copies_kernel, nb),
        in_specs=[
            pl.BlockSpec(memory_space=pltpu.SMEM),
            pl.BlockSpec(memory_space=pltpu.VMEM),
        ],
        out_specs=pl.BlockSpec(memory_space=pltpu.VMEM),
        out_shape=pltpu.VMEM((count, rows, nb * COL), BF),
        compiler_params=LIMIT,
    )(at, projections)


def flip_x(v, bits):
    return lax.ppermute(v, "x", [(i ^ bits, i) for i in range(4)])


def flip_y(v, bits):
    return lax.ppermute(v, ("yh", "yl"), [(i ^ bits, i) for i in range(4)])


def flip_core(v):
    return lax.ppermute(v, "core", [(0, 1), (1, 0)])


def f32(v):
    return v.astype(F32)


def shards(particles, projections, ctf, group_ids):
    n, f = particles.shape
    rows = projections.shape[0]
    nz = lax.axis_size("z")
    poses = rows * nz * 2
    inverse = 4.0 / math.sqrt(f)
    factor = poses / (n * 16 * 2 * nz)
    core = lax.axis_index("core")
    odd = lax.axis_index("x") % 2
    parity = core[None].astype(jnp.int32)
    half = odd[None].astype(jnp.int32)
    ids = group_ids[None, :]

    nb = f // BLK // 2
    copies = copies_call((2 * core + odd)[None].astype(jnp.int32), projections, nb, nz)
    own = lax.all_to_all(copies, "z", 0, 0).reshape(poses // 2, nb * COL)

    w_own = weighted_call(parity, ids, ctf, in_hbm(particles))
    ids_oth = flip_core(ids)
    w_recv = weighted_call(parity, ids_oth, ctf, in_hbm(flip_core(particles)))
    ids_all = jnp.concatenate([ids, ids_oth], axis=1)
    own, w_own, w_recv, ids_all = lax.optimization_barrier((own, w_own, w_recv, ids_all))
    w_own, w_recv = in_hbm(w_own), in_hbm(w_recv)

    mid = nb * COL // 2
    cols = [own[:, :mid], own[:, mid:]]
    by_y = [flip_y(v, b) for v, b in zip(cols, (1, 3))]
    by_x = [flip_x(v, b) for v, b in zip(cols, (1, 3))]
    both = [
        [flip_x(by_y[i][:, : mid // 2], b), flip_y(by_x[i][:, mid // 2 :], b)] for i, b in enumerate((1, 3))
    ]
    at = jnp.concatenate([half, parity, lax.axis_index("yl")[None].astype(jnp.int32)])
    own = jnp.concatenate([own, jnp.concatenate(by_y, axis=1)], axis=0)
    oth = [jnp.concatenate([by_x[i], jnp.concatenate(both[i], axis=1)], axis=0) for i in range(2)]

    s0 = score_call(half, parity, w_own, w_recv, [own], ctf)
    s1 = score_call(1 - half, parity, w_own, w_recv, oth, ctf)
    mine = s0 + s1
    log_norm, weights, mass = softmax_call(inverse, ids_all, mine, flip_core(mine))
    part = gradient_call(at, weights, mass, w_own, w_recv, own, jnp.concatenate(oth, axis=1), ctf)
    part = part.reshape(16, poses // 2, BLK)
    part, log_norm = lax.optimization_barrier((part, log_norm[:, 0]))
    part = lax.all_to_all(part, ("yh", "yl", "x"), 0, 0)
    last = jnp.sum(f32(part), axis=0).astype(BF).reshape(nz, rows, BLK)
    parts = lax.all_to_all(last, "z", 0, 0)
    out = factor * jnp.sum(f32(parts), axis=0)
    return out, log_norm


def in_hbm(v):
    return pltpu.with_memory_space_constraint(v, pltpu.HBM)


def solution(mesh):
    fine = jax.sharding.Mesh(mesh.devices.reshape(2, 4, 2, 2, 8), NAMES)
    grp, pose = ("yh", "x", "core"), ("yl", "z")
    return jax.shard_map(
        shards,
        mesh=fine,
        in_specs=(P(grp + pose, None), P(pose, None), P(), P(grp + pose)),
        out_specs=(P(pose, grp), P(grp + pose)),
        check_vma=False,
    )
```

time: 125 us -> 111 us (0.89)
  blocking collectives: 0 us -> 43.9 us
  waiting for transfers between devices: 46.5 us -> 8.85 us
  local copies, waits for them, and re-layouts: 16.2 us -> 1.78 us
  starting transfers between devices: 32.5 us -> 21.5 us
  Pallas kernels: 24.5 us -> 30.7 us
    all_to_all x0 -> x2, blocking collectives: none -> 43.9 us  [the longest x1 32.1 us: shards(): part = lax.all_to_all(part, ('yh', 'yl', 'x'), 0, 0)]
    all_to_all x4 -> x1, waiting for transfers between devices: 40.6 us -> 4.6 us  [shards(): own = lax.all_to_all(copies, 'z', 0, 0).reshape(poses // 2, nb * COL)]
    all_to_all x4 -> x1, starting transfers between devices: 28.1 us -> 8.47 us  [shards(): own = lax.all_to_all(copies, 'z', 0, 0).reshape(poses // 2, nb * COL)]
    unnamed x13 -> x12, local copies, waits for them, and re-layouts: 10.7 us -> 1.03 us
    ppermute x0 -> x4, starting transfers between devices: none -> 7.12 us  [flip_y(): return lax.ppermute(v, ('yh', 'yl'), [(i ^ bits, i) for i in range(4)])]
    pallas_call x2, Pallas kernels: 7.65 us -> 12.6 us  [weighted_call(): pl.pallas_call(weighted_kernel, grid_spec=pltpu.PrefetchScalarGridSpec(nu...]
    ppermute x3 -> x4, waiting for transfers between devices: 3.39 us -> 0.67 us  [flip_x(): return lax.ppermute(v, 'x', [(i ^ bits, i) for i in range(4)])]
    reshape x2 -> x0, local copies, waits for them, and re-layouts: 2.07 us -> none  [the longest x1 1.83 us: shards(): ctf.reshape(ctf.shape[0], nb, 2, 2, COL)]
  transfers between devices with their start and end apart: 11 -> 12, of which waited for: 8 -> 5; matrix products, arithmetic and copies ran while one was open for 5% -> 2% of each run, Pallas kernels for 13% -> 16%
where the time goes in v3:
time: 111 us
  blocking collectives  43.9 us (40%)
  Pallas kernels  30.7 us (28%)
  starting transfers between devices  21.5 us (19%)
  waiting for transfers between devices  8.85 us (8%)
  other arithmetic  3.35 us (3%)
  local copies, waits for them, and re-layouts  1.78 us (2%)
    all_to_all x1, blocking collectives, shards(): part = lax.all_to_all(part, ('yh', 'yl', 'x'), 0, 0)  32.1 us
    pallas_call x2, Pallas kernels, weighted_call(): pl.pallas_call(weighted_kernel, grid_spec=pltpu.PrefetchScalarGridSpec(nu...  12.6 us
    all_to_all x1, blocking collectives, shards(): parts = lax.all_to_all(last, 'z', 0, 0)  11.8 us
    pallas_call x2, Pallas kernels, score_call(): pl.pallas_call(score_kernel, grid_spec=pltpu.PrefetchScalarGridSpec(num_s...  9.48 us
    all_to_all x1, starting transfers between devices, shards(): own = lax.all_to_all(copies, 'z', 0, 0).reshape(poses // 2, nb * COL)  8.47 us
    pallas_call x1, Pallas kernels, gradient_call(): pl.pallas_call(gradient_kernel, grid_spec=pltpu.PrefetchScalarGridSpec(nu...  7.2 us
    ppermute x4, starting transfers between devices, flip_y(): return lax.ppermute(v, ('yh', 'yl'), [(i ^ bits, i) for i in range(4)])  7.12 us
    ppermute x4, starting transfers between devices, flip_x(): return lax.ppermute(v, 'x', [(i ^ bits, i) for i in range(4)])  5.55 us
  transfers between devices with their start and end apart: 12, of which 5 were waited for; matrix products, arithmetic and copies ran while one was open for 2% of the time, Pallas kernels for 16%

profile of v3, /device:TPU:2, one launch (start us, length us, event | category | flops | bytes accessed | tf_op | source)
XLA Modules:
  0.0 111.0 jit_solution(15550059900364891130)
XLA Ops:
  0.6 0.0 copy-start
  0.6 0.1 collective-permute-start.1
  0.8 0.0 copy-start.1
  0.8 1.0 copy-done.1
  1.8 0.8 shard_map.59
  2.6 8.5 %all-to-all-start = ((bf16[8,8,4096]{2,1,0:T(8,128)(2,1)}), bf16[8,8,4096]{2,1,0:T(8,128)(2,1)S(1)}, u32[]{:S(2)}, u32[]{:S(2)}) async-start(bf16[8,8,4096]{2,1,0:T(8,128)(2,1)} %shard_map.59), calls=%async_computation | async-start | bytes 1048576 | tf_op jit(solution)/shard_map/all_to_all | solution.py:260
  11.1 0.7 broadcast_in_dim.19.ids_ref
  11.8 0.1 collective-permute-start
  11.9 0.0 copy-done
  11.9 6.3 %shard_map.60.wa_ref = bf16[2,320,4096]{2,1,0:T(8,128)(2,1)} custom-call(s32[1]{0:T(128)} %bitcast.1.par_ref, s32[1,320]{1,0:T(1,128)S(1)} %broadcast_in_dim.19.ids_ref, bf16[32,16384]{1,0:T(8,128)(2,1)S(1)} %copy-done, bf16[32,16384]{1,0:T(8,128)(2,1)S(1)} %copy-done, bf16[320,16384]{1,0:T(8,128)(2,1)} %x1_ref.1, bf16[320,16384]{1,0:T(8,128)(2,1)} %x1_ref.1), custom_call_target="tpu_custom_call" | custom-call | tf_op jit(solution)/shard_map/pallas_call | solution.py:56
  18.2 0.0 collective-permute-done.ids_ref
  18.2 0.1 pad_add_fusion.ids_ref
  18.3 0.0 collective-permute-done.1.x0_ref.x1_ref
  18.3 6.3 %shard_map.61.wb_ref = bf16[2,320,4096]{2,1,0:T(8,128)(2,1)} custom-call(s32[1]{0:T(128)} %bitcast.1.par_ref, s32[1,320]{1,0:T(1,128)S(1)} %collective-permute-done.ids_ref, bf16[32,16384]{1,0:T(8,128)(2,1)S(1)} %copy-done, bf16[32,16384]{1,0:T(8,128)(2,1)S(1)} %copy-done, bf16[320,16384]{1,0:T(8,128)(2,1)} %collective-permute-done.1.x0_ref.x1_ref, ...), custom_call_target="tpu_custom_call" | custom-call | tf_op jit(solution)/shard_map/pallas_call | solution.py:56
  24.6 4.6 %all-to-all-done = bf16[8,8,4096]{2,1,0:T(8,128)(2,1)S(1)} async-done(((bf16[8,8,4096]{2,1,0:T(8,128)(2,1)}), bf16[8,8,4096]{2,1,0:T(8,128)(2,1)S(1)}, u32[]{:S(2)}, u32[]{:S(2)}) %all-to-all-start) | async-done | bytes 524320 | tf_op jit(solution)/shard_map/all_to_all | solution.py:260
  29.3 1.7 %collective-permute-start.2 = (bf16[64,2048]{1,0:T(8,128)(2,1)S(1)}, bf16[64,2048]{1,0:T(8,128)(2,1)S(1)}, u32[]{:S(2)}, u32[]{:S(2)}) collective-permute-start(bf16[64,2048]{1,0:T(8,128)(2,1)S(1)} %get-tuple-element.20), channel_id=1, source_target_pairs={{8,0},{0,8},{136,128},{128,136},{9,1},{1,9},{137,129},{129,137},{1... | collective-permute-start | bytes 786440 | tf_op jit(solution)/shard_map/ppermute | solution.py:234
  30.9 0.5 collective-permute-start.4
  31.5 2.2 %collective-permute-start.3 = (bf16[64,2048]{1,0:T(8,128)(2,1)S(1)}, bf16[64,2048]{1,0:T(8,128)(2,1)S(1)}, u32[]{:S(2)}, u32[]{:S(2)}) collective-permute-start(bf16[64,2048]{1,0:T(8,128)(2,1)S(1)} %get-tuple-element.21), channel_id=1, source_target_pairs={{136,0},{128,8},{8,128},{0,136},{137,1},{129,9},{9,129},{1,137},{1... | collective-permute-start | bytes 786440 | tf_op jit(solution)/shard_map/ppermute | solution.py:234
  33.6 2.2 %collective-permute-start.7 = (bf16[64,2048]{1,0:T(8,128)(2,1)S(1)}, bf16[64,2048]{1,0:T(8,128)(2,1)S(1)}, u32[]{:S(2)}, u32[]{:S(2)}) collective-permute-start(bf16[64,2048]{1,0:T(8,128)(2,1)S(1)} %get-tuple-element.21), channel_id=1, source_target_pairs={{96,0},{64,32},{32,64},{0,96},{97,1},{65,33},{33,65},{1,97},{98,2}... | collective-permute-start | bytes 786440 | tf_op jit(solution)/shard_map/ppermute | solution.py:230
  35.8 0.1 pad_add_fusion.2.at_ref
  35.9 0.1 pad_add_fusion.3.at_ref
  35.9 0.1 pad_add_fusion.1.at_ref
  36.0 1.6 %collective-permute-done.2 = bf16[64,2048]{1,0:T(8,128)(2,1)S(1)} collective-permute-done((bf16[64,2048]{1,0:T(8,128)(2,1)S(1)}, bf16[64,2048]{1,0:T(8,128)(2,1)S(1)}, u32[]{:S(2)}, u32[]{:S(2)}) %collective-permute-start.2) | collective-permute-done | bytes 262176 | tf_op jit(solution)/shard_map/ppermute | solution.py:234
  37.6 0.0 copy-start.4
  37.6 0.6 collective-permute-start.5
  38.2 0.7 collective-permute-done.4
  38.9 1.0 collective-permute-start.6
  39.9 0.4 collective-permute-done.3
  40.4 0.0 copy-start.5
  40.4 2.2 %collective-permute-start.8 = (bf16[64,1024]{1,0:T(8,128)(2,1)S(1)}, bf16[64,1024]{1,0:T(8,128)(2,1)S(1)}, u32[]{:S(2)}, u32[]{:S(2)}) collective-permute-start(bf16[64,1024]{1,0:T(8,128)(2,1)S(1)} %slice.26), channel_id=1, source_target_pairs={{96,0},{64,32},{32,64},{0,96},{97,1},{65,33},{33,65},{1,97},{98,2}... | collective-permute-start | bytes 393224 | tf_op jit(solution)/shard_map/ppermute | solution.py:230
  42.6 0.0 collective-permute-done.7
  42.6 0.0 copy-start.2
  42.6 0.0 copy-done.4
  42.6 0.0 copy-done.5
  42.6 2.3 %collective-permute-start.9 = (bf16[64,1024]{1,0:T(8,128)(2,1)S(1)}, bf16[64,1024]{1,0:T(8,128)(2,1)S(1)}, u32[]{:S(2)}, u32[]{:S(2)}) collective-permute-start(bf16[64,1024]{1,0:T(8,128)(2,1)S(1)} %slice.27), channel_id=1, source_target_pairs={{136,0},{128,8},{8,128},{0,136},{137,1},{129,9},{9,129},{1,137},{1... | collective-permute-start | bytes 393224 | tf_op jit(solution)/shard_map/ppermute | solution.py:234
  44.9 1.1 maximum_maximum_fusion.p0_ref.p1_ref
  46.0 4.7 %shard_map.62 = f32[672,128]{1,0:T(8,128)S(1)} custom-call(s32[2]{0:T(128)S(1)} %pad_add_fusion.2.at_ref, bf16[2,320,4096]{2,1,0:T(8,128)(2,1)} %shard_map.60.wa_ref, bf16[2,320,4096]{2,1,0:T(8,128)(2,1)} %shard_map.61.wb_ref, bf16[128,4096]{1,0:T(8,128)(2,1)S(1)} %maximum_maximum_fusion.p0_ref.p1_ref, ...), custom_call_target="tpu_custom_call" | custom-call | tf_op jit(solution)/shard_map/pallas_call | solution.py:117
  50.8 0.0 collective-permute-done.8
  50.8 0.0 collective-permute-done.9
  50.8 0.0 copy-done.2
  50.8 0.0 collective-permute-done.5
  50.9 0.0 collective-permute-done.6
  50.9 0.0 copy-start.3
  50.9 4.7 %shard_map.63 = f32[672,128]{1,0:T(8,128)S(1)} custom-call(s32[2]{0:T(128)S(1)} %pad_add_fusion.3.at_ref, bf16[2,320,4096]{2,1,0:T(8,128)(2,1)} %shard_map.60.wa_ref, bf16[2,320,4096]{2,1,0:T(8,128)(2,1)} %shard_map.61.wb_ref, bf16[128,2048]{1,0:T(8,128)(2,1)S(1)} %maximum_maximum_fusion.2.p0_ref, bf16[128,2048]{1,0:T(8,128)(2,1)S(1)} %maximum_maximum_fusion.3.p1_ref, ...), custom_call_target="tpu_custom_call" | custom-call | tf_op jit(solution)/shard_map/pallas_call | solution.py:117
  55.7 0.1 collective-permute-start.10
  55.8 0.0 copy-done.3
  55.8 0.1 maximum_maximum_fusion.1.p1_ref
  55.9 1.6 %collective-permute-done.10.r_ref = f32[672,128]{1,0:T(8,128)S(1)} collective-permute-done((f32[672,128]{1,0:T(8,128)S(1)}, f32[672,128]{1,0:T(8,128)S(1)}, u32[]{:S(2)}, u32[]{:S(2)}) %collective-permute-start.10) | collective-permute-done | bytes 344096 | tf_op jit(solution)/shard_map/ppermute | solution.py:238
  57.4 0.6 shard_map.64
  58.1 0.7 reduce.1
  58.8 7.2 %shard_map.65 = bf16[2,2,4,64,1024]{4,3,2,1,0:T(8,128)(2,1)S(1)} custom-call(s32[3]{0:T(128)S(1)} %pad_add_fusion.1.at_ref, bf16[640,128]{1,0:T(8,128)(2,1)S(1)} %get-tuple-element.15.w_ref, bf16[160,128]{1,0:T(8,128)(2,1)S(1)} %get-tuple-element.16.mass_ref, bf16[2,320,4096]{2,1,0:T(8,128)(2,1)} %shard_map.60.wa_ref, ...), custom_call_target="tpu_custom_call" | custom-call | tf_op jit(solution)/shard_map/pallas_call | solution.py:194
  66.0 32.1 %all_to_all.15 = bf16[16,64,1024]{2,1,0:T(8,128)(2,1)S(1)} all-to-all(bf16[16,64,1024]{2,1,0:T(8,128)(2,1)S(1)} %bitcast.7), channel_id=1, replica_groups=mesh['yh'=2,'x'=4,'core'=2,'yl'=2,'z'=8] {'yh','yl','x'}, dimensions={0} | all-to-all | bytes 4194304 | tf_op jit(solution)/shard_map/all_to_all | solution.py:287
  98.1 0.4 reduce_sum.21
  98.5 11.8 %all_to_all.16 = bf16[8,8,1024]{2,1,0:T(8,128)(2,1)S(1)} all-to-all(bf16[8,8,1024]{2,1,0:T(8,128)(2,1)S(1)} %bitcast.10), channel_id=1, replica_groups=mesh['yh'=2,'x'=4,'core'=2,'yl'=2,'z'=8] {'z'}, dimensions={0} | all-to-all | bytes 262144 | tf_op jit(solution)/shard_map/all_to_all | solution.py:289
  110.4 0.6 broadcast_multiply_fusion
  (9 shorter events, 0.2 us)
Async XLA Ops:
  0.6 11.3 %copy-start = (bf16[32,16384]{1,0:T(8,128)(2,1)S(1)}, bf16[32,16384]{1,0:T(8,128)(2,1)}, u32[]{:S(2)}) copy-start(bf16[32,16384]{1,0:T(8,128)(2,1)} %c3.5) | copy-start | bytes 3145732
  0.6 17.6 %collective-permute-start.1 = (bf16[320,16384]{1,0:T(8,128)(2,1)}, bf16[320,16384]{1,0:T(8,128)(2,1)}, u32[]{:S(2)}, u32[]{:S(2)}) collective-permute-start(bf16[320,16384]{1,0:T(8,128)(2,1)} %x1_ref.1), channel_id=1, source_target_pairs={{0,16},{16,0},{1,17},{17,1},{2,18},{18,2},{3,19},{19,3},{4,20},{20... | collective-permute-start | bytes 31457288 | tf_op jit(solution)/shard_map/ppermute | solution.py:238
  0.8 1.0 copy-start.1
  2.6 26.6 %all-to-all-start = ((bf16[8,8,4096]{2,1,0:T(8,128)(2,1)}), bf16[8,8,4096]{2,1,0:T(8,128)(2,1)S(1)}, u32[]{:S(2)}, u32[]{:S(2)}) async-start(bf16[8,8,4096]{2,1,0:T(8,128)(2,1)} %shard_map.59), calls=%async_computation | async-start | bytes 1048576 | tf_op jit(solution)/shard_map/all_to_all | solution.py:260
  11.8 6.5 %collective-permute-start = (s32[1,320]{1,0:T(1,128)S(1)}, s32[1,320]{1,0:T(1,128)S(1)}, u32[]{:S(2)}, u32[]{:S(2)}) collective-permute-start(s32[1,320]{1,0:T(1,128)S(1)} %broadcast_in_dim.19.ids_ref), channel_id=1, source_target_pairs={{0,16},{16,0},{1,17},{17,1},{2,18},{18,2},{3,19},{19,3},{4,20},{20... | collective-permute-start | bytes 3848 | tf_op jit(solution)/shard_map/ppermute | solution.py:238
  29.3 8.3 %collective-permute-start.2 = (bf16[64,2048]{1,0:T(8,128)(2,1)S(1)}, bf16[64,2048]{1,0:T(8,128)(2,1)S(1)}, u32[]{:S(2)}, u32[]{:S(2)}) collective-permute-start(bf16[64,2048]{1,0:T(8,128)(2,1)S(1)} %get-tuple-element.20), channel_id=1, source_target_pairs={{8,0},{0,8},{136,128},{128,136},{9,1},{1,9},{137,129},{129,137},{1... | collective-permute-start | bytes 786440 | tf_op jit(solution)/shard_map/ppermute | solution.py:234
  30.9 8.0 %collective-permute-start.4 = (bf16[64,2048]{1,0:T(8,128)(2,1)S(1)}, bf16[64,2048]{1,0:T(8,128)(2,1)S(1)}, u32[]{:S(2)}, u32[]{:S(2)}) collective-permute-start(bf16[64,2048]{1,0:T(8,128)(2,1)S(1)} %get-tuple-element.20), channel_id=1, source_target_pairs={{32,0},{0,32},{96,64},{64,96},{33,1},{1,33},{97,65},{65,97},{34,2}... | collective-permute-start | bytes 786440 | tf_op jit(solution)/shard_map/ppermute | solution.py:230
  31.5 8.9 %collective-permute-start.3 = (bf16[64,2048]{1,0:T(8,128)(2,1)S(1)}, bf16[64,2048]{1,0:T(8,128)(2,1)S(1)}, u32[]{:S(2)}, u32[]{:S(2)}) collective-permute-start(bf16[64,2048]{1,0:T(8,128)(2,1)S(1)} %get-tuple-element.21), channel_id=1, source_target_pairs={{136,0},{128,8},{8,128},{0,136},{137,1},{129,9},{9,129},{1,137},{1... | collective-permute-start | bytes 786440 | tf_op jit(solution)/shard_map/ppermute | solution.py:234
  33.6 9.0 %collective-permute-start.7 = (bf16[64,2048]{1,0:T(8,128)(2,1)S(1)}, bf16[64,2048]{1,0:T(8,128)(2,1)S(1)}, u32[]{:S(2)}, u32[]{:S(2)}) collective-permute-start(bf16[64,2048]{1,0:T(8,128)(2,1)S(1)} %get-tuple-element.21), channel_id=1, source_target_pairs={{96,0},{64,32},{32,64},{0,96},{97,1},{65,33},{33,65},{1,97},{98,2}... | collective-permute-start | bytes 786440 | tf_op jit(solution)/shard_map/ppermute | solution.py:230
  37.6 5.0 %copy-start.4 = (bf16[64,2048]{1,0:T(8,128)(2,1)}, bf16[64,2048]{1,0:T(8,128)(2,1)S(1)}, u32[]{:S(2)}) copy-start(bf16[64,2048]{1,0:T(8,128)(2,1)S(1)} %collective-permute-done.2) | copy-start | bytes 786436
  37.6 13.2 %collective-permute-start.5 = (bf16[64,1024]{1,0:T(8,128)(2,1)S(1)}, bf16[64,1024]{1,0:T(8,128)(2,1)S(1)}, u32[]{:S(2)}, u32[]{:S(2)}) collective-permute-start(bf16[64,1024]{1,0:T(8,128)(2,1)S(1)} %slice.24), channel_id=1, source_target_pairs={{32,0},{0,32},{96,64},{64,96},{33,1},{1,33},{97,65},{65,97},{34,2}... | collective-permute-start | bytes 393224 | tf_op jit(solution)/shard_map/ppermute | solution.py:230
  38.9 12.0 %collective-permute-start.6 = (bf16[64,1024]{1,0:T(8,128)(2,1)S(1)}, bf16[64,1024]{1,0:T(8,128)(2,1)S(1)}, u32[]{:S(2)}, u32[]{:S(2)}) collective-permute-start(bf16[64,1024]{1,0:T(8,128)(2,1)S(1)} %slice.25), channel_id=1, source_target_pairs={{8,0},{0,8},{136,128},{128,136},{9,1},{1,9},{137,129},{129,137},{1... | collective-permute-start | bytes 393224 | tf_op jit(solution)/shard_map/ppermute | solution.py:234
  40.4 2.3 %copy-start.5 = (bf16[64,2048]{1,0:T(8,128)(2,1)}, bf16[64,2048]{1,0:T(8,128)(2,1)S(1)}, u32[]{:S(2)}) copy-start(bf16[64,2048]{1,0:T(8,128)(2,1)S(1)} %collective-permute-done.3) | copy-start | bytes 786436
  40.4 10.4 %collective-permute-start.8 = (bf16[64,1024]{1,0:T(8,128)(2,1)S(1)}, bf16[64,1024]{1,0:T(8,128)(2,1)S(1)}, u32[]{:S(2)}, u32[]{:S(2)}) collective-permute-start(bf16[64,1024]{1,0:T(8,128)(2,1)S(1)} %slice.26), channel_id=1, source_target_pairs={{96,0},{64,32},{32,64},{0,96},{97,1},{65,33},{33,65},{1,97},{98,2}... | collective-permute-start | bytes 393224 | tf_op jit(solution)/shard_map/ppermute | solution.py:230
  42.6 8.2 %copy-start.2 = (bf16[64,2048]{1,0:T(8,128)(2,1)}, bf16[64,2048]{1,0:T(8,128)(2,1)S(1)}, u32[]{:S(2)}) copy-start(bf16[64,2048]{1,0:T(8,128)(2,1)S(1)} %collective-permute-done.7) | copy-start | bytes 786436
  42.6 8.1 %collective-permute-start.9 = (bf16[64,1024]{1,0:T(8,128)(2,1)S(1)}, bf16[64,1024]{1,0:T(8,128)(2,1)S(1)}, u32[]{:S(2)}, u32[]{:S(2)}) collective-permute-start(bf16[64,1024]{1,0:T(8,128)(2,1)S(1)} %slice.27), channel_id=1, source_target_pairs={{136,0},{128,8},{8,128},{0,136},{137,1},{129,9},{9,129},{1,137},{1... | collective-permute-start | bytes 393224 | tf_op jit(solution)/shard_map/ppermute | solution.py:234
  50.9 4.9 %copy-start.3 = (bf16[64,2048]{1,0:T(8,128)(2,1)S(1)}, bf16[64,2048]{1,0:T(8,128)(2,1)}, u32[]{:S(2)}) copy-start(bf16[64,2048]{1,0:T(8,128)(2,1)} %copy-done.2) | copy-start | bytes 786436
  55.7 1.7 %collective-permute-start.10 = (f32[672,128]{1,0:T(8,128)S(1)}, f32[672,128]{1,0:T(8,128)S(1)}, u32[]{:S(2)}, u32[]{:S(2)}) collective-permute-start(f32[672,128]{1,0:T(8,128)S(1)} %add.12.s_ref), channel_id=1, source_target_pairs={{0,16},{16,0},{1,17},{17,1},{2,18},{18,2},{3,19},{19,3},{4,20},{20... | collective-permute-start | bytes 1032200 | tf_op jit(solution)/shard_map/ppermute | solution.py:238

commit v4 on v3

--- a/solution.py
+++ b/solution.py
@@ -257,7 +257,8 @@
 
     nb = f // BLK // 2
     copies = copies_call((2 * core + odd)[None].astype(jnp.int32), projections, nb, nz)
-    own = lax.all_to_all(copies, "z", 0, 0).reshape(poses // 2, nb * COL)
+    up = [list(range(nz)), list(range(2 * nz - 1, nz - 1, -1))]
+    own = lax.all_to_all(copies, ("core", "z"), 0, 0, axis_index_groups=up)
 
     w_own = weighted_call(parity, ids, ctf, in_hbm(particles))
     ids_oth = flip_core(ids)
@@ -265,6 +266,7 @@
     ids_all = jnp.concatenate([ids, ids_oth], axis=1)
     own, w_own, w_recv, ids_all = lax.optimization_barrier((own, w_own, w_recv, ids_all))
     w_own, w_recv = in_hbm(w_own), in_hbm(w_recv)
+    own = jnp.where(core == 1, own[::-1], own).reshape(poses // 2, nb * COL)
 
     mid = nb * COL // 2
     cols = [own[:, :mid], own[:, mid:]]
@@ -286,7 +288,7 @@
     part, log_norm = lax.optimization_barrier((part, log_norm[:, 0]))
     part = lax.all_to_all(part, ("yh", "yl", "x"), 0, 0)
     last = jnp.sum(f32(part), axis=0).astype(BF).reshape(nz, rows, BLK)
-    parts = lax.all_to_all(last, "z", 0, 0)
+    parts = lax.all_to_all(last[::-1], "z", 0, 0, axis_index_groups=[list(range(nz))[::-1]])
     out = factor * jnp.sum(f32(parts), axis=0)
     return out, log_norm
 

time: 111 us -> 109 us (0.982)
  waiting for transfers between devices: 8.85 us -> 4.26 us
  blocking collectives: 43.9 us -> 45.5 us
    all_to_all x1, waiting for transfers between devices: 4.6 us -> 0.6 us  [shards(): own = lax.all_to_all(copies, ('core', 'z'), 0, 0, axis_index_groups=up)]
    all_to_all x1, blocking collectives: 11.8 us -> 13.4 us  [shards(): lax.all_to_all(last[::-1], 'z', 0, 0, axis_index_groups=[list(range(nz))[...]
  transfers between devices with their start and end apart: 12 -> 12, of which waited for: 5 -> 5; matrix products, arithmetic and copies ran while one was open for 2% -> 2% of each run, Pallas kernels for 16% -> 17%
where the time goes in v4:
time: 109 us
  blocking collectives  45.5 us (42%)
  Pallas kernels  30.7 us (28%)
  starting transfers between devices  22.3 us (20%)
  waiting for transfers between devices  4.26 us (4%)
  other arithmetic  3.44 us (3%)
  local copies, waits for them, and re-layouts  1.8 us (2%)
    all_to_all x1, blocking collectives, shards(): part = lax.all_to_all(part, ('yh', 'yl', 'x'), 0, 0)  32.1 us
    all_to_all x1, blocking collectives, shards(): lax.all_to_all(last[::-1], 'z', 0, 0, axis_index_groups=[list(range(nz))[...  13.4 us
    pallas_call x2, Pallas kernels, weighted_call(): pl.pallas_call(weighted_kernel, grid_spec=pltpu.PrefetchScalarGridSpec(nu...  12.6 us
    pallas_call x2, Pallas kernels, score_call(): pl.pallas_call(score_kernel, grid_spec=pltpu.PrefetchScalarGridSpec(num_s...  9.48 us
    all_to_all x1, starting transfers between devices, shards(): own = lax.all_to_all(copies, ('core', 'z'), 0, 0, axis_index_groups=up)  8.47 us
    pallas_call x1, Pallas kernels, gradient_call(): pl.pallas_call(gradient_kernel, grid_spec=pltpu.PrefetchScalarGridSpec(nu...  7.2 us
    ppermute x4, starting transfers between devices, flip_y(): return lax.ppermute(v, ('yh', 'yl'), [(i ^ bits, i) for i in range(4)])  7.09 us
    ppermute x4, starting transfers between devices, flip_x(): return lax.ppermute(v, 'x', [(i ^ bits, i) for i in range(4)])  5.55 us
  transfers between devices with their start and end apart: 12, of which 5 were waited for; matrix products, arithmetic and copies ran while one was open for 2% of the time, Pallas kernels for 17%

profile of v4, /device:TPU:2, one launch (start us, length us, event | category | flops | bytes accessed | tf_op | source)
XLA Modules:
  0.0 108.9 jit_solution(5448090939078561252)
XLA Ops:
  0.6 0.0 copy-start
  0.6 0.1 collective-permute-start.1
  0.8 0.0 copy-start.1
  0.8 1.0 copy-done.1
  1.8 0.8 shard_map.59
  2.6 8.5 %all-to-all-start = ((bf16[8,8,4096]{2,1,0:T(8,128)(2,1)}), bf16[8,8,4096]{2,1,0:T(8,128)(2,1)S(1)}, u32[]{:S(2)}, u32[]{:S(2)}) async-start(bf16[8,8,4096]{2,1,0:T(8,128)(2,1)} %shard_map.59), calls=%async_computation | async-start | bytes 1048576 | tf_op jit(solution)/shard_map/all_to_all | solution.py:261
  11.1 0.7 broadcast_in_dim.19.ids_ref
  11.8 1.0 collective-permute-start
  12.7 0.0 copy-done
  12.7 6.3 %shard_map.60.wa_ref = bf16[2,320,4096]{2,1,0:T(8,128)(2,1)} custom-call(s32[1]{0:T(128)} %bitcast.1.par_ref, s32[1,320]{1,0:T(1,128)S(1)} %broadcast_in_dim.19.ids_ref, bf16[32,16384]{1,0:T(8,128)(2,1)S(1)} %copy-done, bf16[32,16384]{1,0:T(8,128)(2,1)S(1)} %copy-done, bf16[320,16384]{1,0:T(8,128)(2,1)} %x1_ref.1, bf16[320,16384]{1,0:T(8,128)(2,1)} %x1_ref.1), custom_call_target="tpu_custom_call" | custom-call | tf_op jit(solution)/shard_map/pallas_call | solution.py:56
  19.0 0.0 collective-permute-done.ids_ref
  19.0 0.1 pad_add_fusion.ids_ref
  19.1 0.0 collective-permute-done.1.x0_ref.x1_ref
  19.1 6.3 %shard_map.61.wb_ref = bf16[2,320,4096]{2,1,0:T(8,128)(2,1)} custom-call(s32[1]{0:T(128)} %bitcast.1.par_ref, s32[1,320]{1,0:T(1,128)S(1)} %collective-permute-done.ids_ref, bf16[32,16384]{1,0:T(8,128)(2,1)S(1)} %copy-done, bf16[32,16384]{1,0:T(8,128)(2,1)S(1)} %copy-done, bf16[320,16384]{1,0:T(8,128)(2,1)} %collective-permute-done.1.x0_ref.x1_ref, ...), custom_call_target="tpu_custom_call" | custom-call | tf_op jit(solution)/shard_map/pallas_call | solution.py:56
  25.4 0.6 all-to-all-done
  26.0 0.1 fusion
  26.2 1.7 %collective-permute-start.2 = (bf16[64,2048]{1,0:T(8,128)(2,1)S(1)}, bf16[64,2048]{1,0:T(8,128)(2,1)S(1)}, u32[]{:S(2)}, u32[]{:S(2)}) collective-permute-start(bf16[64,2048]{1,0:T(8,128)(2,1)S(1)} %get-tuple-element.20), channel_id=1, source_target_pairs={{8,0},{0,8},{136,128},{128,136},{9,1},{1,9},{137,129},{129,137},{1... | collective-permute-start | bytes 786440 | tf_op jit(solution)/shard_map/ppermute | solution.py:234
  27.8 0.5 collective-permute-start.4
  28.4 2.2 %collective-permute-start.3 = (bf16[64,2048]{1,0:T(8,128)(2,1)S(1)}, bf16[64,2048]{1,0:T(8,128)(2,1)S(1)}, u32[]{:S(2)}, u32[]{:S(2)}) collective-permute-start(bf16[64,2048]{1,0:T(8,128)(2,1)S(1)} %get-tuple-element.21), channel_id=1, source_target_pairs={{136,0},{128,8},{8,128},{0,136},{137,1},{129,9},{9,129},{1,137},{1... | collective-permute-start | bytes 786440 | tf_op jit(solution)/shard_map/ppermute | solution.py:234
  30.5 2.2 %collective-permute-start.7 = (bf16[64,2048]{1,0:T(8,128)(2,1)S(1)}, bf16[64,2048]{1,0:T(8,128)(2,1)S(1)}, u32[]{:S(2)}, u32[]{:S(2)}) collective-permute-start(bf16[64,2048]{1,0:T(8,128)(2,1)S(1)} %get-tuple-element.21), channel_id=1, source_target_pairs={{96,0},{64,32},{32,64},{0,96},{97,1},{65,33},{33,65},{1,97},{98,2}... | collective-permute-start | bytes 786440 | tf_op jit(solution)/shard_map/ppermute | solution.py:230
  32.7 0.1 pad_add_fusion.2.at_ref
  32.8 0.1 pad_add_fusion.3.at_ref
  32.8 0.1 pad_add_fusion.1.at_ref
  32.9 1.0 collective-permute-done.2
  33.9 0.0 copy-start.4
  33.9 0.6 collective-permute-start.5
  34.5 0.7 collective-permute-done.4
  35.2 1.0 collective-permute-start.6
  36.2 0.4 collective-permute-done.3
  36.7 0.0 copy-start.5
  36.7 2.2 %collective-permute-start.8 = (bf16[64,1024]{1,0:T(8,128)(2,1)S(1)}, bf16[64,1024]{1,0:T(8,128)(2,1)S(1)}, u32[]{:S(2)}, u32[]{:S(2)}) collective-permute-start(bf16[64,1024]{1,0:T(8,128)(2,1)S(1)} %slice.28), channel_id=1, source_target_pairs={{96,0},{64,32},{32,64},{0,96},{97,1},{65,33},{33,65},{1,97},{98,2}... | collective-permute-start | bytes 393224 | tf_op jit(solution)/shard_map/ppermute | solution.py:230
  38.9 0.0 collective-permute-done.7
  38.9 0.0 copy-start.2
  38.9 0.0 copy-done.4
  38.9 0.0 copy-done.5
  39.0 2.3 %collective-permute-start.9 = (bf16[64,1024]{1,0:T(8,128)(2,1)S(1)}, bf16[64,1024]{1,0:T(8,128)(2,1)S(1)}, u32[]{:S(2)}, u32[]{:S(2)}) collective-permute-start(bf16[64,1024]{1,0:T(8,128)(2,1)S(1)} %slice.29), channel_id=1, source_target_pairs={{136,0},{128,8},{8,128},{0,136},{137,1},{129,9},{9,129},{1,137},{1... | collective-permute-start | bytes 393224 | tf_op jit(solution)/shard_map/ppermute | solution.py:234
  41.2 1.1 %maximum_maximum_fusion.p0_ref.p1_ref = bf16[128,4096]{1,0:T(8,128)(2,1)S(1)} fusion(bf16[64,2048]{1,0:T(8,128)(2,1)} %copy-done.5, bf16[64,2048]{1,0:T(8,128)(2,1)} %copy-done.4, bf16[64,4096]{1,0:T(8,128)(2,1)S(1)} %fusion), kind=kLoop, calls=%fused_computation | loop fusion | flops 3145728 | bytes 2097152 | tf_op jit(solution)/shard_map/concatenate | solution.py:279
  42.3 4.8 %shard_map.62 = f32[672,128]{1,0:T(8,128)S(1)} custom-call(s32[2]{0:T(128)S(1)} %pad_add_fusion.2.at_ref, bf16[2,320,4096]{2,1,0:T(8,128)(2,1)} %shard_map.60.wa_ref, bf16[2,320,4096]{2,1,0:T(8,128)(2,1)} %shard_map.61.wb_ref, bf16[128,4096]{1,0:T(8,128)(2,1)S(1)} %maximum_maximum_fusion.p0_ref.p1_ref, ...), custom_call_target="tpu_custom_call" | custom-call | tf_op jit(solution)/shard_map/pallas_call | solution.py:117
  47.1 0.0 collective-permute-done.8
  47.1 0.0 collective-permute-done.9
  47.1 0.0 copy-done.2
  47.1 0.0 collective-permute-done.5
  47.2 0.0 collective-permute-done.6
  47.2 0.0 copy-start.3
  47.2 4.7 %shard_map.63 = f32[672,128]{1,0:T(8,128)S(1)} custom-call(s32[2]{0:T(128)S(1)} %pad_add_fusion.3.at_ref, bf16[2,320,4096]{2,1,0:T(8,128)(2,1)} %shard_map.60.wa_ref, bf16[2,320,4096]{2,1,0:T(8,128)(2,1)} %shard_map.61.wb_ref, bf16[128,2048]{1,0:T(8,128)(2,1)S(1)} %maximum_maximum_fusion.2.p0_ref, bf16[128,2048]{1,0:T(8,128)(2,1)S(1)} %maximum_maximum_fusion.3.p1_ref, ...), custom_call_target="tpu_custom_call" | custom-call | tf_op jit(solution)/shard_map/pallas_call | solution.py:117
  52.0 0.1 collective-permute-start.10
  52.1 0.0 copy-done.3
  52.1 0.1 maximum_maximum_fusion.1.p1_ref
  52.2 1.6 %collective-permute-done.10.r_ref = f32[672,128]{1,0:T(8,128)S(1)} collective-permute-done((f32[672,128]{1,0:T(8,128)S(1)}, f32[672,128]{1,0:T(8,128)S(1)}, u32[]{:S(2)}, u32[]{:S(2)}) %collective-permute-start.10) | collective-permute-done | bytes 344096 | tf_op jit(solution)/shard_map/ppermute | solution.py:238
  53.8 0.6 shard_map.64
  54.4 0.7 reduce.1
  55.1 7.2 %shard_map.65 = bf16[2,2,4,64,1024]{4,3,2,1,0:T(8,128)(2,1)S(1)} custom-call(s32[3]{0:T(128)S(1)} %pad_add_fusion.1.at_ref, bf16[640,128]{1,0:T(8,128)(2,1)S(1)} %get-tuple-element.15.w_ref, bf16[160,128]{1,0:T(8,128)(2,1)S(1)} %get-tuple-element.16.mass_ref, bf16[2,320,4096]{2,1,0:T(8,128)(2,1)} %shard_map.60.wa_ref, ...), custom_call_target="tpu_custom_call" | custom-call | tf_op jit(solution)/shard_map/pallas_call | solution.py:194
  62.3 32.1 %all_to_all.15 = bf16[16,64,1024]{2,1,0:T(8,128)(2,1)S(1)} all-to-all(bf16[16,64,1024]{2,1,0:T(8,128)(2,1)S(1)} %bitcast.8), channel_id=1, replica_groups=mesh['yh'=2,'x'=4,'core'=2,'yl'=2,'z'=8] {'yh','yl','x'}, dimensions={0} | all-to-all | bytes 4194304 | tf_op jit(solution)/shard_map/all_to_all | solution.py:289
  94.4 0.4 reduce_sum.21
  94.8 13.4 %all_to_all.16 = bf16[8,8,1024]{2,1,0:T(8,128)(2,1)S(1)} all-to-all(bf16[8,8,1024]{2,1,0:T(8,128)(2,1)S(1)} %rev.7), channel_id=1, replica_groups={{7,6,5,4,3,2,1,0},{15,14,13,12,11,10,9,8},{23,22,21,20,19,18,17,16},{31..., dimensions={0} | all-to-all | bytes 262144 | tf_op jit(solution)/shard_map/all_to_all | solution.py:291
  108.3 0.6 broadcast_multiply_fusion
  (10 shorter events, 0.2 us)
Async XLA Ops:
  0.6 12.1 %copy-start = (bf16[32,16384]{1,0:T(8,128)(2,1)S(1)}, bf16[32,16384]{1,0:T(8,128)(2,1)}, u32[]{:S(2)}) copy-start(bf16[32,16384]{1,0:T(8,128)(2,1)} %c3.5) | copy-start | bytes 3145732
  0.6 18.5 %collective-permute-start.1 = (bf16[320,16384]{1,0:T(8,128)(2,1)}, bf16[320,16384]{1,0:T(8,128)(2,1)}, u32[]{:S(2)}, u32[]{:S(2)}) collective-permute-start(bf16[320,16384]{1,0:T(8,128)(2,1)} %x1_ref.1), channel_id=1, source_target_pairs={{0,16},{16,0},{1,17},{17,1},{2,18},{18,2},{3,19},{19,3},{4,20},{20... | collective-permute-start | bytes 31457288 | tf_op jit(solution)/shard_map/ppermute | solution.py:238
  0.8 1.0 copy-start.1
  2.6 23.4 %all-to-all-start = ((bf16[8,8,4096]{2,1,0:T(8,128)(2,1)}), bf16[8,8,4096]{2,1,0:T(8,128)(2,1)S(1)}, u32[]{:S(2)}, u32[]{:S(2)}) async-start(bf16[8,8,4096]{2,1,0:T(8,128)(2,1)} %shard_map.59), calls=%async_computation | async-start | bytes 1048576 | tf_op jit(solution)/shard_map/all_to_all | solution.py:261
  11.8 7.3 %collective-permute-start = (s32[1,320]{1,0:T(1,128)S(1)}, s32[1,320]{1,0:T(1,128)S(1)}, u32[]{:S(2)}, u32[]{:S(2)}) collective-permute-start(s32[1,320]{1,0:T(1,128)S(1)} %broadcast_in_dim.19.ids_ref), channel_id=1, source_target_pairs={{0,16},{16,0},{1,17},{17,1},{2,18},{18,2},{3,19},{19,3},{4,20},{20... | collective-permute-start | bytes 3848 | tf_op jit(solution)/shard_map/ppermute | solution.py:238
  26.2 7.7 %collective-permute-start.2 = (bf16[64,2048]{1,0:T(8,128)(2,1)S(1)}, bf16[64,2048]{1,0:T(8,128)(2,1)S(1)}, u32[]{:S(2)}, u32[]{:S(2)}) collective-permute-start(bf16[64,2048]{1,0:T(8,128)(2,1)S(1)} %get-tuple-element.20), channel_id=1, source_target_pairs={{8,0},{0,8},{136,128},{128,136},{9,1},{1,9},{137,129},{129,137},{1... | collective-permute-start | bytes 786440 | tf_op jit(solution)/shard_map/ppermute | solution.py:234
  27.8 7.4 %collective-permute-start.4 = (bf16[64,2048]{1,0:T(8,128)(2,1)S(1)}, bf16[64,2048]{1,0:T(8,128)(2,1)S(1)}, u32[]{:S(2)}, u32[]{:S(2)}) collective-permute-start(bf16[64,2048]{1,0:T(8,128)(2,1)S(1)} %get-tuple-element.20), channel_id=1, source_target_pairs={{32,0},{0,32},{96,64},{64,96},{33,1},{1,33},{97,65},{65,97},{34,2}... | collective-permute-start | bytes 786440 | tf_op jit(solution)/shard_map/ppermute | solution.py:230
  28.4 8.3 %collective-permute-start.3 = (bf16[64,2048]{1,0:T(8,128)(2,1)S(1)}, bf16[64,2048]{1,0:T(8,128)(2,1)S(1)}, u32[]{:S(2)}, u32[]{:S(2)}) collective-permute-start(bf16[64,2048]{1,0:T(8,128)(2,1)S(1)} %get-tuple-element.21), channel_id=1, source_target_pairs={{136,0},{128,8},{8,128},{0,136},{137,1},{129,9},{9,129},{1,137},{1... | collective-permute-start | bytes 786440 | tf_op jit(solution)/shard_map/ppermute | solution.py:234
  30.5 8.4 %collective-permute-start.7 = (bf16[64,2048]{1,0:T(8,128)(2,1)S(1)}, bf16[64,2048]{1,0:T(8,128)(2,1)S(1)}, u32[]{:S(2)}, u32[]{:S(2)}) collective-permute-start(bf16[64,2048]{1,0:T(8,128)(2,1)S(1)} %get-tuple-element.21), channel_id=1, source_target_pairs={{96,0},{64,32},{32,64},{0,96},{97,1},{65,33},{33,65},{1,97},{98,2}... | collective-permute-start | bytes 786440 | tf_op jit(solution)/shard_map/ppermute | solution.py:230
  33.9 5.0 %copy-start.4 = (bf16[64,2048]{1,0:T(8,128)(2,1)}, bf16[64,2048]{1,0:T(8,128)(2,1)S(1)}, u32[]{:S(2)}) copy-start(bf16[64,2048]{1,0:T(8,128)(2,1)S(1)} %collective-permute-done.2) | copy-start | bytes 786436
  33.9 13.2 %collective-permute-start.5 = (bf16[64,1024]{1,0:T(8,128)(2,1)S(1)}, bf16[64,1024]{1,0:T(8,128)(2,1)S(1)}, u32[]{:S(2)}, u32[]{:S(2)}) collective-permute-start(bf16[64,1024]{1,0:T(8,128)(2,1)S(1)} %slice.26), channel_id=1, source_target_pairs={{32,0},{0,32},{96,64},{64,96},{33,1},{1,33},{97,65},{65,97},{34,2}... | collective-permute-start | bytes 393224 | tf_op jit(solution)/shard_map/ppermute | solution.py:230
  35.2 11.9 %collective-permute-start.6 = (bf16[64,1024]{1,0:T(8,128)(2,1)S(1)}, bf16[64,1024]{1,0:T(8,128)(2,1)S(1)}, u32[]{:S(2)}, u32[]{:S(2)}) collective-permute-start(bf16[64,1024]{1,0:T(8,128)(2,1)S(1)} %slice.27), channel_id=1, source_target_pairs={{8,0},{0,8},{136,128},{128,136},{9,1},{1,9},{137,129},{129,137},{1... | collective-permute-start | bytes 393224 | tf_op jit(solution)/shard_map/ppermute | solution.py:234
  36.7 2.3 %copy-start.5 = (bf16[64,2048]{1,0:T(8,128)(2,1)}, bf16[64,2048]{1,0:T(8,128)(2,1)S(1)}, u32[]{:S(2)}) copy-start(bf16[64,2048]{1,0:T(8,128)(2,1)S(1)} %collective-permute-done.3) | copy-start | bytes 786436
  36.7 10.4 %collective-permute-start.8 = (bf16[64,1024]{1,0:T(8,128)(2,1)S(1)}, bf16[64,1024]{1,0:T(8,128)(2,1)S(1)}, u32[]{:S(2)}, u32[]{:S(2)}) collective-permute-start(bf16[64,1024]{1,0:T(8,128)(2,1)S(1)} %slice.28), channel_id=1, source_target_pairs={{96,0},{64,32},{32,64},{0,96},{97,1},{65,33},{33,65},{1,97},{98,2}... | collective-permute-start | bytes 393224 | tf_op jit(solution)/shard_map/ppermute | solution.py:230
  38.9 8.2 %copy-start.2 = (bf16[64,2048]{1,0:T(8,128)(2,1)}, bf16[64,2048]{1,0:T(8,128)(2,1)S(1)}, u32[]{:S(2)}) copy-start(bf16[64,2048]{1,0:T(8,128)(2,1)S(1)} %collective-permute-done.7) | copy-start | bytes 786436
  39.0 8.1 %collective-permute-start.9 = (bf16[64,1024]{1,0:T(8,128)(2,1)S(1)}, bf16[64,1024]{1,0:T(8,128)(2,1)S(1)}, u32[]{:S(2)}, u32[]{:S(2)}) collective-permute-start(bf16[64,1024]{1,0:T(8,128)(2,1)S(1)} %slice.29), channel_id=1, source_target_pairs={{136,0},{128,8},{8,128},{0,136},{137,1},{129,9},{9,129},{1,137},{1... | collective-permute-start | bytes 393224 | tf_op jit(solution)/shard_map/ppermute | solution.py:234
  47.2 4.9 %copy-start.3 = (bf16[64,2048]{1,0:T(8,128)(2,1)S(1)}, bf16[64,2048]{1,0:T(8,128)(2,1)}, u32[]{:S(2)}) copy-start(bf16[64,2048]{1,0:T(8,128)(2,1)} %copy-done.2) | copy-start | bytes 786436
  52.0 1.7 %collective-permute-start.10 = (f32[672,128]{1,0:T(8,128)S(1)}, f32[672,128]{1,0:T(8,128)S(1)}, u32[]{:S(2)}, u32[]{:S(2)}) collective-permute-start(f32[672,128]{1,0:T(8,128)S(1)} %add.12.s_ref), channel_id=1, source_target_pairs={{0,16},{16,0},{1,17},{17,1},{2,18},{18,2},{3,19},{19,3},{4,20},{20... | collective-permute-start | bytes 1032200 | tf_op jit(solution)/shard_map/ppermute | solution.py:238

commit v5 on v4

--- a/solution.py
+++ b/solution.py
@@ -285,12 +285,12 @@
     log_norm, weights, mass = softmax_call(inverse, ids_all, mine, flip_core(mine))
     part = gradient_call(at, weights, mass, w_own, w_recv, own, jnp.concatenate(oth, axis=1), ctf)
     part = part.reshape(16, poses // 2, BLK)
-    part, log_norm = lax.optimization_barrier((part, log_norm[:, 0]))
     part = lax.all_to_all(part, ("yh", "yl", "x"), 0, 0)
     last = jnp.sum(f32(part), axis=0).astype(BF).reshape(nz, rows, BLK)
     parts = lax.all_to_all(last[::-1], "z", 0, 0, axis_index_groups=[list(range(nz))[::-1]])
+    parts, log_norm = lax.optimization_barrier((parts, log_norm))
     out = factor * jnp.sum(f32(parts), axis=0)
-    return out, log_norm
+    return out, log_norm[:, 0]
 
 
 def in_hbm(v):

time: 109 us -> 108 us (level)
  transfers between devices with their start and end apart: 12 -> 12, of which waited for: 5 -> 5; matrix products, arithmetic and copies ran while one was open for 2% -> 1% of each run, Pallas kernels for 17% -> 17%
where the time goes in v5:
time: 108 us
  blocking collectives  45.5 us (42%)
  Pallas kernels  30.8 us (29%)
  starting transfers between devices  22.3 us (21%)
  waiting for transfers between devices  4.27 us (4%)
  other arithmetic  2.41 us (2%)
  local copies, waits for them, and re-layouts  1.79 us (2%)
    all_to_all x1, blocking collectives, shards(): part = lax.all_to_all(part, ('yh', 'yl', 'x'), 0, 0)  32.1 us
    all_to_all x1, blocking collectives, shards(): lax.all_to_all(last[::-1], 'z', 0, 0, axis_index_groups=[list(range(nz))[...  13.4 us
    pallas_call x2, Pallas kernels, weighted_call(): pl.pallas_call(weighted_kernel, grid_spec=pltpu.PrefetchScalarGridSpec(nu...  12.6 us
    pallas_call x2, Pallas kernels, score_call(): pl.pallas_call(score_kernel, grid_spec=pltpu.PrefetchScalarGridSpec(num_s...  9.49 us
    all_to_all x1, starting transfers between devices, shards(): own = lax.all_to_all(copies, ('core', 'z'), 0, 0, axis_index_groups=up)  8.47 us
    pallas_call x1, Pallas kernels, gradient_call(): pl.pallas_call(gradient_kernel, grid_spec=pltpu.PrefetchScalarGridSpec(nu...  7.21 us
    ppermute x4, starting transfers between devices, flip_y(): return lax.ppermute(v, ('yh', 'yl'), [(i ^ bits, i) for i in range(4)])  7.1 us
    ppermute x4, starting transfers between devices, flip_x(): return lax.ppermute(v, 'x', [(i ^ bits, i) for i in range(4)])  5.55 us
  transfers between devices with their start and end apart: 12, of which 5 were waited for; matrix products, arithmetic and copies ran while one was open for 1% of the time, Pallas kernels for 17%

profile of v5, /device:TPU:2, one launch (start us, length us, event | category | flops | bytes accessed | tf_op | source)
XLA Modules:
  0.0 107.9 jit_solution(13315764353203262409)
XLA Ops:
  0.6 0.0 copy-start
  0.6 0.1 collective-permute-start.1
  0.8 0.0 copy-start.1
  0.8 1.0 copy-done.1
  1.8 0.8 shard_map.59
  2.6 8.5 %all-to-all-start = ((bf16[8,8,4096]{2,1,0:T(8,128)(2,1)}), bf16[8,8,4096]{2,1,0:T(8,128)(2,1)S(1)}, u32[]{:S(2)}, u32[]{:S(2)}) async-start(bf16[8,8,4096]{2,1,0:T(8,128)(2,1)} %shard_map.59), calls=%async_computation | async-start | bytes 1048576 | tf_op jit(solution)/shard_map/all_to_all | solution.py:261
  11.1 0.7 broadcast_in_dim.19.ids_ref
  11.8 1.0 collective-permute-start
  12.7 0.0 copy-done
  12.7 6.3 %shard_map.60.wa_ref = bf16[2,320,4096]{2,1,0:T(8,128)(2,1)} custom-call(s32[1]{0:T(128)} %bitcast.1.par_ref, s32[1,320]{1,0:T(1,128)S(1)} %broadcast_in_dim.19.ids_ref, bf16[32,16384]{1,0:T(8,128)(2,1)S(1)} %copy-done, bf16[32,16384]{1,0:T(8,128)(2,1)S(1)} %copy-done, bf16[320,16384]{1,0:T(8,128)(2,1)} %x1_ref.1, bf16[320,16384]{1,0:T(8,128)(2,1)} %x1_ref.1), custom_call_target="tpu_custom_call" | custom-call | tf_op jit(solution)/shard_map/pallas_call | solution.py:56
  19.0 0.0 collective-permute-done.ids_ref
  19.0 0.1 pad_add_fusion.ids_ref
  19.1 0.0 collective-permute-done.1.x0_ref.x1_ref
  19.1 6.3 %shard_map.61.wb_ref = bf16[2,320,4096]{2,1,0:T(8,128)(2,1)} custom-call(s32[1]{0:T(128)} %bitcast.1.par_ref, s32[1,320]{1,0:T(1,128)S(1)} %collective-permute-done.ids_ref, bf16[32,16384]{1,0:T(8,128)(2,1)S(1)} %copy-done, bf16[32,16384]{1,0:T(8,128)(2,1)S(1)} %copy-done, bf16[320,16384]{1,0:T(8,128)(2,1)} %collective-permute-done.1.x0_ref.x1_ref, ...), custom_call_target="tpu_custom_call" | custom-call | tf_op jit(solution)/shard_map/pallas_call | solution.py:56
  25.4 0.6 all-to-all-done
  26.0 0.1 fusion
  26.2 1.7 %collective-permute-start.2 = (bf16[64,2048]{1,0:T(8,128)(2,1)S(1)}, bf16[64,2048]{1,0:T(8,128)(2,1)S(1)}, u32[]{:S(2)}, u32[]{:S(2)}) collective-permute-start(bf16[64,2048]{1,0:T(8,128)(2,1)S(1)} %get-tuple-element.20), channel_id=1, source_target_pairs={{8,0},{0,8},{136,128},{128,136},{9,1},{1,9},{137,129},{129,137},{1... | collective-permute-start | bytes 786440 | tf_op jit(solution)/shard_map/ppermute | solution.py:234
  27.8 0.5 collective-permute-start.4
  28.4 2.2 %collective-permute-start.3 = (bf16[64,2048]{1,0:T(8,128)(2,1)S(1)}, bf16[64,2048]{1,0:T(8,128)(2,1)S(1)}, u32[]{:S(2)}, u32[]{:S(2)}) collective-permute-start(bf16[64,2048]{1,0:T(8,128)(2,1)S(1)} %get-tuple-element.21), channel_id=1, source_target_pairs={{136,0},{128,8},{8,128},{0,136},{137,1},{129,9},{9,129},{1,137},{1... | collective-permute-start | bytes 786440 | tf_op jit(solution)/shard_map/ppermute | solution.py:234
  30.6 2.2 %collective-permute-start.7 = (bf16[64,2048]{1,0:T(8,128)(2,1)S(1)}, bf16[64,2048]{1,0:T(8,128)(2,1)S(1)}, u32[]{:S(2)}, u32[]{:S(2)}) collective-permute-start(bf16[64,2048]{1,0:T(8,128)(2,1)S(1)} %get-tuple-element.21), channel_id=1, source_target_pairs={{96,0},{64,32},{32,64},{0,96},{97,1},{65,33},{33,65},{1,97},{98,2}... | collective-permute-start | bytes 786440 | tf_op jit(solution)/shard_map/ppermute | solution.py:230
  32.7 0.1 pad_add_fusion.2.at_ref
  32.8 0.1 pad_add_fusion.3.at_ref
  32.9 0.1 pad_add_fusion.1.at_ref
  32.9 1.0 collective-permute-done.2
  33.9 0.6 collective-permute-start.5
  34.6 0.7 collective-permute-done.4
  35.2 1.0 collective-permute-start.6
  36.2 0.4 collective-permute-done.3
  36.7 2.2 %collective-permute-start.8 = (bf16[64,1024]{1,0:T(8,128)(2,1)S(1)}, bf16[64,1024]{1,0:T(8,128)(2,1)S(1)}, u32[]{:S(2)}, u32[]{:S(2)}) collective-permute-start(bf16[64,1024]{1,0:T(8,128)(2,1)S(1)} %slice.28), channel_id=1, source_target_pairs={{96,0},{64,32},{32,64},{0,96},{97,1},{65,33},{33,65},{1,97},{98,2}... | collective-permute-start | bytes 393224 | tf_op jit(solution)/shard_map/ppermute | solution.py:230
  38.9 0.0 collective-permute-done.7
  38.9 2.3 %collective-permute-start.9 = (bf16[64,1024]{1,0:T(8,128)(2,1)S(1)}, bf16[64,1024]{1,0:T(8,128)(2,1)S(1)}, u32[]{:S(2)}, u32[]{:S(2)}) collective-permute-start(bf16[64,1024]{1,0:T(8,128)(2,1)S(1)} %slice.29), channel_id=1, source_target_pairs={{136,0},{128,8},{8,128},{0,136},{137,1},{129,9},{9,129},{1,137},{1... | collective-permute-start | bytes 393224 | tf_op jit(solution)/shard_map/ppermute | solution.py:234
  41.2 0.1 maximum_maximum_fusion.p0_ref.p1_ref
  41.3 4.7 %shard_map.62 = f32[672,128]{1,0:T(8,128)S(1)} custom-call(s32[2]{0:T(128)S(1)} %pad_add_fusion.2.at_ref, bf16[2,320,4096]{2,1,0:T(8,128)(2,1)} %shard_map.60.wa_ref, bf16[2,320,4096]{2,1,0:T(8,128)(2,1)} %shard_map.61.wb_ref, bf16[128,4096]{1,0:T(8,128)(2,1)S(1)} %maximum_maximum_fusion.p0_ref.p1_ref, ...), custom_call_target="tpu_custom_call" | custom-call | tf_op jit(solution)/shard_map/pallas_call | solution.py:117
  46.0 0.0 collective-permute-done.8
  46.1 0.0 collective-permute-done.9
  46.1 0.0 collective-permute-done.5
  46.1 0.0 collective-permute-done.6
  46.2 4.7 %shard_map.63 = f32[672,128]{1,0:T(8,128)S(1)} custom-call(s32[2]{0:T(128)S(1)} %pad_add_fusion.3.at_ref, bf16[2,320,4096]{2,1,0:T(8,128)(2,1)} %shard_map.60.wa_ref, bf16[2,320,4096]{2,1,0:T(8,128)(2,1)} %shard_map.61.wb_ref, bf16[128,2048]{1,0:T(8,128)(2,1)S(1)} %maximum_maximum_fusion.2.p0_ref, bf16[128,2048]{1,0:T(8,128)(2,1)S(1)} %maximum_maximum_fusion.3.p1_ref, ...), custom_call_target="tpu_custom_call" | custom-call | tf_op jit(solution)/shard_map/pallas_call | solution.py:117
  51.0 0.1 collective-permute-start.10
  51.1 0.1 maximum_maximum_fusion.1.p1_ref
  51.2 1.6 %collective-permute-done.10.r_ref = f32[672,128]{1,0:T(8,128)S(1)} collective-permute-done((f32[672,128]{1,0:T(8,128)S(1)}, f32[672,128]{1,0:T(8,128)S(1)}, u32[]{:S(2)}, u32[]{:S(2)}) %collective-permute-start.10) | collective-permute-done | bytes 344096 | tf_op jit(solution)/shard_map/ppermute | solution.py:238
  52.7 0.6 shard_map.64
  53.3 7.2 %shard_map.65 = bf16[2,2,4,64,1024]{4,3,2,1,0:T(8,128)(2,1)S(1)} custom-call(s32[3]{0:T(128)S(1)} %pad_add_fusion.1.at_ref, bf16[640,128]{1,0:T(8,128)(2,1)S(1)} %get-tuple-element.15.w_ref, bf16[160,128]{1,0:T(8,128)(2,1)S(1)} %get-tuple-element.16.mass_ref, bf16[2,320,4096]{2,1,0:T(8,128)(2,1)} %shard_map.60.wa_ref, ...), custom_call_target="tpu_custom_call" | custom-call | tf_op jit(solution)/shard_map/pallas_call | solution.py:194
  60.5 32.1 %all_to_all.15 = bf16[16,64,1024]{2,1,0:T(8,128)(2,1)S(1)} all-to-all(bf16[16,64,1024]{2,1,0:T(8,128)(2,1)S(1)} %bitcast.8), channel_id=1, replica_groups=mesh['yh'=2,'x'=4,'core'=2,'yl'=2,'z'=8] {'yh','yl','x'}, dimensions={0} | all-to-all | bytes 4194304 | tf_op jit(solution)/shard_map/all_to_all | solution.py:288
  92.7 0.4 reduce_sum.21
  93.1 13.4 %all_to_all.16 = bf16[8,8,1024]{2,1,0:T(8,128)(2,1)S(1)} all-to-all(bf16[8,8,1024]{2,1,0:T(8,128)(2,1)S(1)} %rev.7), channel_id=1, replica_groups={{7,6,5,4,3,2,1,0},{15,14,13,12,11,10,9,8},{23,22,21,20,19,18,17,16},{31..., dimensions={0} | all-to-all | bytes 262144 | tf_op jit(solution)/shard_map/all_to_all | solution.py:290
  106.5 0.6 broadcast_multiply_fusion
  107.1 0.7 reduce.1
  (10 shorter events, 0.2 us)
Async XLA Ops:
  0.6 12.1 %copy-start = (bf16[32,16384]{1,0:T(8,128)(2,1)S(1)}, bf16[32,16384]{1,0:T(8,128)(2,1)}, u32[]{:S(2)}) copy-start(bf16[32,16384]{1,0:T(8,128)(2,1)} %c3.5) | copy-start | bytes 3145732
  0.6 18.5 %collective-permute-start.1 = (bf16[320,16384]{1,0:T(8,128)(2,1)}, bf16[320,16384]{1,0:T(8,128)(2,1)}, u32[]{:S(2)}, u32[]{:S(2)}) collective-permute-start(bf16[320,16384]{1,0:T(8,128)(2,1)} %x1_ref.1), channel_id=1, source_target_pairs={{0,16},{16,0},{1,17},{17,1},{2,18},{18,2},{3,19},{19,3},{4,20},{20... | collective-permute-start | bytes 31457288 | tf_op jit(solution)/shard_map/ppermute | solution.py:238
  0.8 1.0 copy-start.1
  2.6 23.4 %all-to-all-start = ((bf16[8,8,4096]{2,1,0:T(8,128)(2,1)}), bf16[8,8,4096]{2,1,0:T(8,128)(2,1)S(1)}, u32[]{:S(2)}, u32[]{:S(2)}) async-start(bf16[8,8,4096]{2,1,0:T(8,128)(2,1)} %shard_map.59), calls=%async_computation | async-start | bytes 1048576 | tf_op jit(solution)/shard_map/all_to_all | solution.py:261
  11.8 7.3 %collective-permute-start = (s32[1,320]{1,0:T(1,128)S(1)}, s32[1,320]{1,0:T(1,128)S(1)}, u32[]{:S(2)}, u32[]{:S(2)}) collective-permute-start(s32[1,320]{1,0:T(1,128)S(1)} %broadcast_in_dim.19.ids_ref), channel_id=1, source_target_pairs={{0,16},{16,0},{1,17},{17,1},{2,18},{18,2},{3,19},{19,3},{4,20},{20... | collective-permute-start | bytes 3848 | tf_op jit(solution)/shard_map/ppermute | solution.py:238
  26.2 7.7 %collective-permute-start.2 = (bf16[64,2048]{1,0:T(8,128)(2,1)S(1)}, bf16[64,2048]{1,0:T(8,128)(2,1)S(1)}, u32[]{:S(2)}, u32[]{:S(2)}) collective-permute-start(bf16[64,2048]{1,0:T(8,128)(2,1)S(1)} %get-tuple-element.20), channel_id=1, source_target_pairs={{8,0},{0,8},{136,128},{128,136},{9,1},{1,9},{137,129},{129,137},{1... | collective-permute-start | bytes 786440 | tf_op jit(solution)/shard_map/ppermute | solution.py:234
  27.8 7.4 %collective-permute-start.4 = (bf16[64,2048]{1,0:T(8,128)(2,1)S(1)}, bf16[64,2048]{1,0:T(8,128)(2,1)S(1)}, u32[]{:S(2)}, u32[]{:S(2)}) collective-permute-start(bf16[64,2048]{1,0:T(8,128)(2,1)S(1)} %get-tuple-element.20), channel_id=1, source_target_pairs={{32,0},{0,32},{96,64},{64,96},{33,1},{1,33},{97,65},{65,97},{34,2}... | collective-permute-start | bytes 786440 | tf_op jit(solution)/shard_map/ppermute | solution.py:230
  28.4 8.3 %collective-permute-start.3 = (bf16[64,2048]{1,0:T(8,128)(2,1)S(1)}, bf16[64,2048]{1,0:T(8,128)(2,1)S(1)}, u32[]{:S(2)}, u32[]{:S(2)}) collective-permute-start(bf16[64,2048]{1,0:T(8,128)(2,1)S(1)} %get-tuple-element.21), channel_id=1, source_target_pairs={{136,0},{128,8},{8,128},{0,136},{137,1},{129,9},{9,129},{1,137},{1... | collective-permute-start | bytes 786440 | tf_op jit(solution)/shard_map/ppermute | solution.py:234
  30.6 8.4 %collective-permute-start.7 = (bf16[64,2048]{1,0:T(8,128)(2,1)S(1)}, bf16[64,2048]{1,0:T(8,128)(2,1)S(1)}, u32[]{:S(2)}, u32[]{:S(2)}) collective-permute-start(bf16[64,2048]{1,0:T(8,128)(2,1)S(1)} %get-tuple-element.21), channel_id=1, source_target_pairs={{96,0},{64,32},{32,64},{0,96},{97,1},{65,33},{33,65},{1,97},{98,2}... | collective-permute-start | bytes 786440 | tf_op jit(solution)/shard_map/ppermute | solution.py:230
  33.9 12.2 %collective-permute-start.5 = (bf16[64,1024]{1,0:T(8,128)(2,1)S(1)}, bf16[64,1024]{1,0:T(8,128)(2,1)S(1)}, u32[]{:S(2)}, u32[]{:S(2)}) collective-permute-start(bf16[64,1024]{1,0:T(8,128)(2,1)S(1)} %slice.26), channel_id=1, source_target_pairs={{32,0},{0,32},{96,64},{64,96},{33,1},{1,33},{97,65},{65,97},{34,2}... | collective-permute-start | bytes 393224 | tf_op jit(solution)/shard_map/ppermute | solution.py:230
  35.2 10.9 %collective-permute-start.6 = (bf16[64,1024]{1,0:T(8,128)(2,1)S(1)}, bf16[64,1024]{1,0:T(8,128)(2,1)S(1)}, u32[]{:S(2)}, u32[]{:S(2)}) collective-permute-start(bf16[64,1024]{1,0:T(8,128)(2,1)S(1)} %slice.27), channel_id=1, source_target_pairs={{8,0},{0,8},{136,128},{128,136},{9,1},{1,9},{137,129},{129,137},{1... | collective-permute-start | bytes 393224 | tf_op jit(solution)/shard_map/ppermute | solution.py:234
  36.7 9.4 %collective-permute-start.8 = (bf16[64,1024]{1,0:T(8,128)(2,1)S(1)}, bf16[64,1024]{1,0:T(8,128)(2,1)S(1)}, u32[]{:S(2)}, u32[]{:S(2)}) collective-permute-start(bf16[64,1024]{1,0:T(8,128)(2,1)S(1)} %slice.28), channel_id=1, source_target_pairs={{96,0},{64,32},{32,64},{0,96},{97,1},{65,33},{33,65},{1,97},{98,2}... | collective-permute-start | bytes 393224 | tf_op jit(solution)/shard_map/ppermute | solution.py:230
  38.9 7.1 %collective-permute-start.9 = (bf16[64,1024]{1,0:T(8,128)(2,1)S(1)}, bf16[64,1024]{1,0:T(8,128)(2,1)S(1)}, u32[]{:S(2)}, u32[]{:S(2)}) collective-permute-start(bf16[64,1024]{1,0:T(8,128)(2,1)S(1)} %slice.29), channel_id=1, source_target_pairs={{136,0},{128,8},{8,128},{0,136},{137,1},{129,9},{9,129},{1,137},{1... | collective-permute-start | bytes 393224 | tf_op jit(solution)/shard_map/ppermute | solution.py:234
  51.0 1.7 %collective-permute-start.10 = (f32[672,128]{1,0:T(8,128)S(1)}, f32[672,128]{1,0:T(8,128)S(1)}, u32[]{:S(2)}, u32[]{:S(2)}) collective-permute-start(f32[672,128]{1,0:T(8,128)S(1)} %add.12.s_ref), channel_id=1, source_target_pairs={{0,16},{16,0},{1,17},{17,1},{2,18},{18,2},{3,19},{19,3},{4,20},{20... | collective-permute-start | bytes 1032200 | tf_op jit(solution)/shard_map/ppermute | solution.py:238
